TPU v7x, 256 devices: a whole 4x4x8 slice. The times are simulated.
256 devices in a mesh: grp: 4 (over x), dev: 64 (over y, z, core).
Axes of the slice: x: 4, y: 4, z: 8, core: 2. Of those that a mesh axis runs over, the one named last changes fastest.
Arguments:
- points: bfloat16 [524288, 256], P(('grp', 'dev')), may hold values from -6 to 6
- ridge: float32 [1024], replicated, may hold values from 0.25 to 2
- landmark_ids: int32 [1024], replicated, may hold values from 0 to 524287, as said below
Outputs:
- features: bfloat16 [524288, 1024], P(('grp', 'dev'))
Inputs may be any that keep to these rules, and one draw needn't show every extreme that they name: `landmark_ids`: sorted ascending, all distinct.
All inputs are finite; a program needn't handle non-finite values.
Results may differ from a plain program's by a relative error of at most 0.0015.
Values may be sent and summed in bfloat16 or wider, within the bound.
A program may use at most 128 MiB of HBM per device.

v0:
```python
import jax
import jax.numpy as jnp
from jax import lax
from jax.sharding import Mesh
from jax.sharding import PartitionSpec as P

GRP_DEV = ("grp", "dev_0", "dev_1", "dev_2")


def one_axis_at_a_time(array, axes):
    for axis in axes:
        array = lax.psum(array, axis)
    return array


def kernel_block(left, right):
    left_sq = jnp.sum(jnp.square(left.astype(jnp.float32)), axis=1)
    right_sq = jnp.sum(jnp.square(right.astype(jnp.float32)), axis=1)
    inner = jnp.dot(left, right.T, preferred_element_type=jnp.float32)
    width = left.shape[1]
    return jnp.exp(-(left_sq[:, None] + right_sq[None, :] - 2.0 * inner) / (2.0 * width))


def shards(points, ridge, landmark_ids):
    count = points.shape[0]
    start = lax.axis_index(GRP_DEV) * count
    offset = landmark_ids - start
    inside = (offset >= 0) & (offset < count)
    picked = points[jnp.clip(offset, 0, count - 1)]
    filled = jnp.where(inside[:, None], picked.astype(jnp.float32), 0.0)
    marks = lax.psum(filled, GRP_DEV).astype(jnp.bfloat16)
    core = kernel_block(marks, marks) + jnp.diag(ridge)
    lower = jnp.linalg.cholesky(core)
    cross = kernel_block(points, marks)
    raw = lax.linalg.triangular_solve(lower, cross, left_side=False, lower=True, transpose_a=True)
    total_rows = count * lax.axis_size(GRP_DEV)
    totals, squares = (
        one_axis_at_a_time(jnp.sum(raw, axis=0), GRP_DEV),
        one_axis_at_a_time(jnp.sum(jnp.square(raw), axis=0), GRP_DEV),
    )
    mean = totals / total_rows
    var = jnp.maximum(squares / total_rows - jnp.square(mean), 0.0)
    centered = raw - mean[None, :]
    return (centered / jnp.sqrt(var + 1e-05)[None, :]).astype(jnp.bfloat16)


def solution(mesh):
    torus = Mesh(
        mesh.devices.reshape(mesh.shape["grp"], 4, 8, 2), ("grp", "dev_0", "dev_1", "dev_2")
    )
    placed = (P(GRP_DEV, None), P(), P())
    return jax.shard_map(
        shards, mesh=torus, in_specs=placed, out_specs=P(GRP_DEV, None), check_vma=False
    )
```

profile of v0, /device:TPU:1, one launch (start us, length us, event | category | flops | bytes accessed | tf_op | source)
XLA Modules:
  0.0 525.0 jit_solution(6520955987927953334)
XLA Ops:
  3.0 4.9 gather_fusion
  8.1 85.5 %all-reduce.6 = bf16[1024,256]{1,0:T(8,128)(2,1)S(1)} all-reduce(f32[1024,256]{1,0:T(8,128)S(1)} %convert_select_fusion), channel_id=1, replica_groups=mesh['grp'=4,'dev_0'=4,'dev_1'=8,'dev_2'=2] {'grp','dev_0','dev_1','dev_2'}, use_global_device_ids=true, to_apply=%region_1.2 | all-reduce | flops 262144 | bytes 1572864 | tf_op jit(solution)/shard_map/psum | solution.py:31
  98.2 5.6 %subtract_negate_fusion = (f32[1024,1024]{0,1:T(8,128)}, f32[1024,1024]{0,1:T(8,128)}, f32[1024,1024]{0,1:T(8,128)}) fusion(f32[1024]{0:T(1024)S(1)} %multiply_reduce_fusion.2, bf16[1024,256]{1,0:T(8,128)(2,1)S(1)} %all-reduce.6), kind=kOutput, calls=%fused_computation.27 | convolution fusion | flops 541065216 | bytes 13111296 | tf_op jit(solution)/shard_map/dot_general | solution.py:19
  103.8 5.4 %copy.5 = f32[1024,1024]{1,0:T(8,128)} copy(f32[1024,1024]{0,1:T(8,128)} %get-tuple-element.82) | data formatting | bytes 8388608 | tf_op jit(solution)/shard_map/neg | solution.py:21
  109.2 5.3 %copy.6 = f32[1024,1024]{1,0:T(8,128)} copy(f32[1024,1024]{0,1:T(8,128)} %get-tuple-element.83) | data formatting | bytes 8388608 | tf_op jit(solution)/shard_map/add | solution.py:21
  114.5 6.3 %fusion.16 = f32[1024,1024]{1,0:T(8,128)S(1)} fusion(f32[1024,1024]{1,0:T(8,128)} %copy.6, f32[1024,1024]{1,0:T(8,128)} %copy.5, f32[1024,1024]{0,1:T(8,128)} %get-tuple-element.84, f32[1024]{0:T(1024)S(1)} %copy-done.5), kind=kLoop, calls=%fused_computation.24 | loop fusion | flops 13631488 | bytes 16781312 | tf_op jit(solution)/shard_map/jit(cholesky)/div | solution.py:33
  122.8 11.7 %cholesky.222 = f32[128,128]{1,0:T(8,128)S(1)} custom-call(f32[128,128]{1,0:T(8,128)S(1)} %cholesky.577), custom_call_target="Cholesky" | custom-call | tf_op jit(solution)/shard_map/jit(cholesky)/cholesky | solution.py:33
  134.6 9.8 %custom-call.62 = f32[1,128,128]{1,2,0:T(8,128)S(1)} custom-call(f32[1,128,128]{2,1,0:T(8,128)S(1)} %get-tuple-element.79), custom_call_target="InvertDiagBlocksLowerTriangular" | custom-call | tf_op jit(solution)/shard_map/jit(cholesky)/cholesky | solution.py:33
  150.8 11.7 %cholesky.243 = f32[128,128]{1,0:T(8,128)S(1)} custom-call(f32[128,128]{1,0:T(8,128)S(1)} %cholesky.581), custom_call_target="Cholesky" | custom-call | tf_op jit(solution)/shard_map/jit(cholesky)/cholesky | solution.py:33
  165.2 10.2 %custom-call.63 = f32[1,128,128]{1,2,0:T(8,128)S(1)} custom-call(f32[1,128,128]{2,1,0:T(8,128)S(1)} %get-tuple-element.76), custom_call_target="InvertDiagBlocksLowerTriangular" | custom-call | tf_op jit(solution)/shard_map/jit(cholesky)/cholesky | solution.py:33
  178.7 11.7 %cholesky.466 = f32[128,128]{1,0:T(8,128)S(1)} custom-call(f32[128,128]{1,0:T(8,128)S(1)} %cholesky.586), custom_call_target="Cholesky" | custom-call | tf_op jit(solution)/shard_map/jit(cholesky)/cholesky | solution.py:33
  192.3 9.8 %custom-call.64 = f32[1,128,128]{1,2,0:T(8,128)S(1)} custom-call(f32[1,128,128]{2,1,0:T(8,128)S(1)} %get-tuple-element.73), custom_call_target="InvertDiagBlocksLowerTriangular" | custom-call | tf_op jit(solution)/shard_map/jit(cholesky)/cholesky | solution.py:33
  205.6 11.9 %cholesky.485 = f32[128,128]{1,0:T(8,128)S(1)} custom-call(f32[128,128]{1,0:T(8,128)S(1)} %cholesky.591), custom_call_target="Cholesky" | custom-call | tf_op jit(solution)/shard_map/jit(cholesky)/cholesky | solution.py:33
  219.4 9.8 %custom-call.65 = f32[1,128,128]{1,2,0:T(8,128)S(1)} custom-call(f32[1,128,128]{2,1,0:T(8,128)S(1)} %get-tuple-element.70), custom_call_target="InvertDiagBlocksLowerTriangular" | custom-call | tf_op jit(solution)/shard_map/jit(cholesky)/cholesky | solution.py:33
  232.6 11.7 %cholesky.504 = f32[128,128]{1,0:T(8,128)S(1)} custom-call(f32[128,128]{1,0:T(8,128)S(1)} %cholesky.596), custom_call_target="Cholesky" | custom-call | tf_op jit(solution)/shard_map/jit(cholesky)/cholesky | solution.py:33
  246.3 9.8 %custom-call.66 = f32[1,128,128]{1,2,0:T(8,128)S(1)} custom-call(f32[1,128,128]{2,1,0:T(8,128)S(1)} %get-tuple-element.67), custom_call_target="InvertDiagBlocksLowerTriangular" | custom-call | tf_op jit(solution)/shard_map/jit(cholesky)/cholesky | solution.py:33
  259.6 11.7 %cholesky.524 = f32[128,128]{1,0:T(8,128)S(1)} custom-call(f32[128,128]{1,0:T(8,128)S(1)} %cholesky.601), custom_call_target="Cholesky" | custom-call | tf_op jit(solution)/shard_map/jit(cholesky)/cholesky | solution.py:33
  273.2 9.8 %custom-call.67 = f32[1,128,128]{1,2,0:T(8,128)S(1)} custom-call(f32[1,128,128]{2,1,0:T(8,128)S(1)} %get-tuple-element.64), custom_call_target="InvertDiagBlocksLowerTriangular" | custom-call | tf_op jit(solution)/shard_map/jit(cholesky)/cholesky | solution.py:33
  286.1 11.7 %cholesky.544 = f32[128,128]{1,0:T(8,128)S(1)} custom-call(f32[128,128]{1,0:T(8,128)S(1)} %cholesky.606), custom_call_target="Cholesky" | custom-call | tf_op jit(solution)/shard_map/jit(cholesky)/cholesky | solution.py:33
  299.8 10.2 %custom-call.68 = f32[1,128,128]{1,2,0:T(8,128)S(1)} custom-call(f32[1,128,128]{2,1,0:T(8,128)S(1)} %get-tuple-element.61), custom_call_target="InvertDiagBlocksLowerTriangular" | custom-call | tf_op jit(solution)/shard_map/jit(cholesky)/cholesky | solution.py:33
  312.6 11.7 %cholesky.562 = f32[128,128]{1,0:T(8,128)S(1)} custom-call(f32[128,128]{1,0:T(8,128)S(1)} %convolution_subtract_fusion.11), custom_call_target="Cholesky" | custom-call | tf_op jit(solution)/shard_map/jit(cholesky)/cholesky | solution.py:33
  326.1 4.9 select_select_fusion
  331.0 22.5 %while.1 = (s32[]{:T(128)}, f32[1024,1024]{1,0:T(8,128)}, s32[8,2]{0,1:T(2,128)S(1)}, f32[8,128,128]{2,1,0:T(8,128)S(1)}, s32[]{:T(128)}) while((s32[]{:T(128)}, f32[1024,1024]{1,0:T(8,128)}, s32[8,2]{0,1:T(2,128)S(1)}, f32[8,128,128]{2,1,0:T(8,128)S(1)}, s32[]{:T(128)}) %tuple.61), condition=%wide.while_cond, body=%wide.while_body.sunk | while | flops 2 | bytes 131189 | solution.py:35
  353.5 78.8 %custom-call.69 = f32[8,128,128]{1,2,0:T(8,128)S(1)} custom-call(f32[8,128,128]{2,1,0:T(8,128)S(1)} %get-tuple-element.12), custom_call_target="InvertDiagBlocksLowerTriangular" | custom-call | tf_op jit(solution)/shard_map/triangular_solve | solution.py:35
  447.8 5.0 fusion.26
  466.4 5.8 %convolution_subtract_fusion.1 = f32[2048,128]{0,1:T(8,128)S(1)} fusion(f32[2048,896]{0,1:T(8,128)S(1)} %get-tuple-element.33, f32[2048,1024]{0,1:T(8,128)S(1)} %bitcast.124, f32[1024,1024]{1,0:T(8,128)} %get-tuple-element.137), kind=kOutput, calls=%fused_computation.38 | convolution fusion | flops 2818834432 | bytes 9895936 | tf_op jit(solution)/shard_map/triangular_solve | solution.py:35
  476.5 9.3 %all-reduce.3 = (f32[1024]{0:T(1024)S(1)}, f32[1024]{0:T(1024)S(1)}) all-reduce(f32[1024]{0:T(1024)S(1)} %get-tuple-element.14, f32[1024]{0:T(1024)S(1)} %get-tuple-element.13), channel_id=1, replica_groups=mesh['grp'=4,'dev_0'=4,'dev_1'=8,'dev_2'=2] {'grp'}, use_global_device_ids=true, to_apply=%region_25.26 | all-reduce | flops 2048 | bytes 16384 | tf_op jit(solution)/shard_map/psum | solution.py:12
  485.8 6.6 %all-reduce.2 = (f32[1024]{0:T(1024)S(1)}, f32[1024]{0:T(1024)S(1)}) all-reduce(f32[1024]{0:T(1024)S(1)} %get-tuple-element.27, f32[1024]{0:T(1024)S(1)} %get-tuple-element.28), channel_id=1, replica_groups=mesh['grp'=4,'dev_0'=4,'dev_1'=8,'dev_2'=2] {'dev_0'}, use_global_device_ids=true, to_apply=%region_26.27 | all-reduce | flops 2048 | bytes 16384 | tf_op jit(solution)/shard_map/psum | solution.py:12
  492.4 12.0 %all-reduce.1 = (f32[1024]{0:T(1024)S(1)}, f32[1024]{0:T(1024)S(1)}) all-reduce(f32[1024]{0:T(1024)S(1)} %get-tuple-element.25, f32[1024]{0:T(1024)S(1)} %get-tuple-element.26), channel_id=1, replica_groups=mesh['grp'=4,'dev_0'=4,'dev_1'=8,'dev_2'=2] {'dev_1'}, use_global_device_ids=true, to_apply=%region_27.28 | all-reduce | flops 2048 | bytes 16384 | tf_op jit(solution)/shard_map/psum | solution.py:12
  504.4 8.4 %all-reduce.4 = (f32[1024]{0:T(1024)S(1)}, f32[1024]{0:T(1024)S(1)}) all-reduce(f32[1024]{0:T(1024)S(1)} %get-tuple-element.23, f32[1024]{0:T(1024)S(1)} %get-tuple-element.24), channel_id=1, replica_groups=mesh['grp'=4,'dev_0'=4,'dev_1'=8,'dev_2'=2] {'dev_2'}, use_global_device_ids=true, to_apply=%region_28.29 | all-reduce | flops 2048 | bytes 16384 | tf_op jit(solution)/shard_map/psum | solution.py:12
  512.8 5.3 %divide_convert_fusion = bf16[2048,1024]{0,1:T(8,128)(2,1)} fusion(f32[2048,1024]{0,1:T(8,128)} %copy-done, f32[1024]{0:T(1024)S(1)} %get-tuple-element.81, f32[1024]{0:T(1024)S(1)} %get-tuple-element.80), kind=kLoop, calls=%fused_computation.7 | loop fusion | flops 6291456 | bytes 12591104 | tf_op jit(solution)/shard_map/convert_element_type | solution.py:44
  518.2 6.4 %copy.7 = bf16[2048,1024]{1,0:T(8,128)(2,1)} copy(bf16[2048,1024]{0,1:T(8,128)(2,1)} %divide_convert_fusion) | data formatting | bytes 8388608 | tf_op jit(solution)/shard_map/convert_element_type | solution.py:44
  (102 shorter events, 100.3 us)
Async XLA Ops:
  3.0 90.9 %copy-start.1 = (bf16[2048,256]{1,0:T(8,128)(2,1)S(1)}, bf16[2048,256]{1,0:T(8,128)(2,1)}, u32[]{:S(2)}) copy-start(bf16[2048,256]{1,0:T(8,128)(2,1)} %param.3) | copy-start | bytes 3145732
  109.2 5.4 %copy-start.5 = (f32[1024]{0:T(1024)S(1)}, f32[1024]{0:T(1024)}, u32[]{:S(2)}) copy-start(f32[1024]{0:T(1024)} %param.4) | copy-start | bytes 12292
  120.8 2.0 copy-start.2
  432.2 5.3 %copy-start.3 = (f32[8,128,128]{1,2,0:T(8,128)}, f32[8,128,128]{1,2,0:T(8,128)S(1)}, u32[]{:S(2)}) copy-start(f32[8,128,128]{1,2,0:T(8,128)S(1)} %custom-call.69) | copy-start | bytes 1572868
  432.3 6.6 %slice-start = ((s8[8388608]{0:T(1024)(128)(4,1)}), s8[4194304]{0:T(1024)(128)(4,1)S(1)}, s32[]{:S(2)}) async-start(s8[8388608]{0:T(1024)(128)(4,1)} %bitcast.123), calls=%async_computation | async-start | bytes 8388608
  435.0 3.8 slice-start.1
  438.8 2.3 copy-start.4
  473.3 3.2 copy-start
where the time goes:
time: 532 us; the launch traced here: 525 us
  other arithmetic  272 us (51%)
  blocking collectives  122 us (23%)
  matrix products  74 us (14%)
  local copies, waits for them, and re-layouts  51 us (10%)
  between operations  5.82 us (1%)
    another operation x30, other arithmetic, shards(): lower = jnp.linalg.cholesky(core)  172 us
    psum x1, blocking collectives, shards(): marks = lax.psum(filled, GRP_DEV).astype(jnp.bfloat16)  85.5 us
    another operation x3, other arithmetic, shards(): lax.linalg.triangular_solve(lower, cross, left_side=False, lower=True, tr...  83.7 us
    another operation x15, matrix products, shards(): lax.linalg.triangular_solve(lower, cross, left_side=False, lower=True, tr...  40.8 us
    psum x4, blocking collectives, one_axis_at_a_time(): array = lax.psum(array, axis)  36.3 us
    another operation x14, matrix products, shards(): lower = jnp.linalg.cholesky(core)  23.2 us
    another operation x24, local copies, waits for them, and re-layouts  22.3 us

commit v1 on v0

v1 whole, which is shorter than its diff:
```python
import functools

import jax
import jax.numpy as jnp
from jax import lax
from jax.experimental import pallas as pl
from jax.experimental.pallas import tpu as pltpu
from jax.sharding import Mesh
from jax.sharding import PartitionSpec as P

GRP_DEV = ("grp", "dev_0", "dev_1", "dev_2")
F32 = jnp.float32
BF16 = jnp.bfloat16
HI = lax.Precision.HIGHEST
BLK = 128
ROWS_STEP = 256
VMEM = pl.BlockSpec(memory_space=pltpu.VMEM)


def lane(x, c):
    return jnp.broadcast_to(x[:, c : c + 1], (8, 128))


def sub(x, k):
    return jnp.broadcast_to(x[k : k + 1, :], (8, 128))


def eliminate64(g1, g2, lane0):
    row = lax.broadcasted_iota(jnp.int32, (8, 128), 0)
    for q in range(8):
        b = [[lane(g1[t], lane0 + 8 * q + c) for t in range(q, 8)] for c in range(8)]
        scale = None
        for k in range(8):
            p = sub(b[k][0], k)
            r = 1.0 / p
            rs = lax.rsqrt(p)
            scale = rs if scale is None else jnp.where(row == k, rs, scale)
            m = [x * r for x in b[k]]
            m[0] = jnp.where(row > k, m[0], 0.0)
            for c in range(k + 1, 8):
                a = sub(b[c][0], k)
                b[c] = [x - y * a for x, y in zip(b[c], m)]
            a1 = sub(g1[q], k)
            a2 = sub(g2[q], k)
            for t in range(q, 8):
                g1[t] = g1[t] - m[t - q] * a1
                g2[t] = g2[t] - m[t - q] * a2
        g1[q] = g1[q] * scale
        g2[q] = g2[q] * scale
    return g1, g2


def dot(a, b):
    return jnp.dot(a, b, preferred_element_type=F32, precision=HI)


def inverse_factor(s, eye):
    rows = lambda x: [x[8 * t : 8 * t + 8] for t in range(8)]
    u, v = eliminate64(rows(s[:64]), rows(eye[:64]), 0)
    u = jnp.concatenate(u, 0)
    v = jnp.concatenate(v, 0)
    ut = u.T[64:128]
    _, v2 = eliminate64(rows(s[64:] - dot(ut, u)), rows(eye[64:] - dot(ut, v)), 64)
    return jnp.concatenate([v] + v2, 0)


def split(x):
    high = x.astype(BF16)
    return high, (x - high.astype(F32)).astype(BF16)


def factor_kernel(marks_ref, ridge_ref, hi_ref, lo_ref, norm_ref, m):
    n, d = marks_ref.shape
    nb = n // BLK
    eye = (
        lax.broadcasted_iota(jnp.int32, (BLK, BLK), 0)
        == lax.broadcasted_iota(jnp.int32, (BLK, BLK), 1)
    ).astype(F32)
    sq = jnp.square(marks_ref[...].astype(F32))
    nr = lax.dot_general(
        jnp.ones((8, d), F32), sq, (((1,), (1,)), ((), ())), preferred_element_type=F32, precision=HI
    )
    norm_ref[...] = nr
    for i in range(nb):
        rows = slice(i * BLK, (i + 1) * BLK)
        blk = marks_ref[rows, :]
        nc = jnp.sum(jnp.square(blk.astype(F32)), axis=1, keepdims=True)
        g = lax.dot_general(blk, marks_ref[...], (((1,), (1,)), ((), ())), preferred_element_type=F32)
        m[rows, :] = jnp.exp((2.0 * g - nc - nr[:1]) * (1.0 / (2.0 * d)))
        m[rows, rows] += eye * ridge_ref[:, rows]

    def step(j, carry):
        o = pl.multiple_of(j * BLK, BLK)
        linv = inverse_factor(m[pl.ds(o, BLK), pl.ds(o, BLK)], eye)
        m[pl.ds(o, BLK), pl.ds(o, BLK)] = eye
        m[pl.ds(o, BLK), :] = dot(linv, m[pl.ds(o, BLK), :])

        def update(i, carry):
            p = pl.multiple_of(i * BLK, BLK)
            ut = m[pl.ds(o, BLK), pl.ds(p, BLK)].T
            m[pl.ds(p, BLK), pl.ds(o, BLK)] = jnp.zeros((BLK, BLK), F32)
            m[pl.ds(p, BLK), :] = m[pl.ds(p, BLK), :] - dot(ut, m[pl.ds(o, BLK), :])
            return carry

        return lax.fori_loop(j + 1, nb, update, carry)

    lax.fori_loop(0, nb, step, 0)
    for i in range(nb):
        rows = slice(i * BLK, (i + 1) * BLK)
        x = m[rows, :]
        x = jnp.where(lax.broadcasted_iota(jnp.int32, x.shape, 1) < (i + 1) * BLK, x, 0.0)
        hi_ref[rows, :], lo_ref[rows, :] = split(x)


def factor(marks, ridge):
    n = marks.shape[0]
    return pl.pallas_call(
        factor_kernel,
        out_shape=[
            jax.ShapeDtypeStruct((n, n), BF16),
            jax.ShapeDtypeStruct((n, n), BF16),
            jax.ShapeDtypeStruct((8, n), F32),
        ],
        in_specs=[VMEM, VMEM],
        out_specs=[VMEM, VMEM, VMEM],
        scratch_shapes=[pltpu.VMEM((n, n), F32)],
        name="factor",
        compiler_params=pltpu.CompilerParams(vmem_limit_bytes=40 << 20),
    )(marks, ridge.reshape(1, n))


def raw_kernel(points_ref, marks_ref, norm_ref, hi_ref, lo_ref, raw_ref, stats_ref):
    d = points_ref.shape[1]
    n = marks_ref.shape[0]
    pts = points_ref[...]
    nc = jnp.sum(jnp.square(pts.astype(F32)), axis=1, keepdims=True)
    g = lax.dot_general(pts, marks_ref[...], (((1,), (1,)), ((), ())), preferred_element_type=F32)
    ch, cl = split(jnp.exp((2.0 * g - nc - norm_ref[:1, :]) * (1.0 / (2.0 * d))))

    @pl.when(pl.program_id(0) == 0)
    def _():
        stats_ref[...] = jnp.zeros_like(stats_ref)

    for j in range(n // 256):
        cols = slice(j * 256, (j + 1) * 256)
        k = (j + 1) * 256
        mul = lambda a, b: lax.dot_general(
            a, b, (((1,), (1,)), ((), ())), preferred_element_type=F32
        )
        x = mul(ch[:, :k], hi_ref[cols, :k])
        x += mul(cl[:, :k], hi_ref[cols, :k])
        x += mul(ch[:, :k], lo_ref[cols, :k])
        raw_ref[:, cols] = x
        stats_ref[0:1, cols] += jnp.sum(x, axis=0, keepdims=True)
        stats_ref[1:2, cols] += jnp.sum(jnp.square(x), axis=0, keepdims=True)


def raw_features(points, marks, norms, hi, lo):
    rows, d = points.shape
    n = marks.shape[0]
    whole = lambda shape: pl.BlockSpec(shape, lambda i: (0, 0), pipeline_mode=pl.Buffered(1))
    return pl.pallas_call(
        raw_kernel,
        grid=(rows // ROWS_STEP,),
        out_shape=[jax.ShapeDtypeStruct((rows, n), F32), jax.ShapeDtypeStruct((8, n), F32)],
        in_specs=[
            pl.BlockSpec((ROWS_STEP, d), lambda i: (i, 0)),
            whole((n, d)),
            whole((8, n)),
            whole((n, n)),
            whole((n, n)),
        ],
        out_specs=[
            pl.BlockSpec((ROWS_STEP, n), lambda i: (i, 0)),
            pl.BlockSpec((8, n), lambda i: (0, 0)),
        ],
        name="raw",
        compiler_params=pltpu.CompilerParams(vmem_limit_bytes=40 << 20),
    )(points, marks, norms, hi, lo)


def shards(points, ridge, landmark_ids):
    count = points.shape[0]
    start = lax.axis_index(GRP_DEV) * count
    offset = landmark_ids - start
    inside = (offset >= 0) & (offset < count)
    picked = points[jnp.clip(offset, 0, count - 1)]
    filled = jnp.where(inside[:, None], picked, jnp.zeros((), BF16))
    marks = lax.psum(filled, GRP_DEV)
    hi, lo, norms = factor(marks, ridge)
    raw, stats = raw_features(points, marks, norms, hi, lo)
    total_rows = count * lax.axis_size(GRP_DEV)
    stats = lax.psum(stats[:2], GRP_DEV) / total_rows
    mean, var = stats[0], jnp.maximum(stats[1] - jnp.square(stats[0]), 0.0)
    return ((raw - mean[None, :]) * lax.rsqrt(var + 1e-05)[None, :]).astype(BF16)


def solution(mesh):
    torus = Mesh(
        mesh.devices.reshape(mesh.shape["grp"], 4, 8, 2), ("grp", "dev_0", "dev_1", "dev_2")
    )
    placed = (P(GRP_DEV, None), P(), P())
    return jax.shard_map(
        shards, mesh=torus, in_specs=placed, out_specs=P(GRP_DEV, None), check_vma=False
    )
```

time: 532 us -> 440 us (0.83); the launches traced: 525 us -> 440 us
  other arithmetic: 272 us -> 9.09 us
  waiting for transfers between devices: 0 us -> 258 us
  matrix products: 74 us -> 0 us
  Pallas kernels: 0 us -> 69.8 us
  blocking collectives: 122 us -> 77.6 us
  local copies, waits for them, and re-layouts: 51 us -> 12 us
  between operations: 5.82 us -> 13.4 us
    psum x0 -> x1, waiting for transfers between devices: none -> 258 us  [shards(): marks = lax.psum(filled, GRP_DEV)]
    another operation x33 -> x0, other arithmetic: 256 us -> none  [the longest x30 172 us: shards(): lower = jnp.linalg.cholesky(core)]
    pallas_call x0 -> x2, Pallas kernels: none -> 69.8 us  [the longest x1 54.9 us: factor(): pl.pallas_call(factor_kernel, out_shape=[jax.ShapeDtypeStruct((n, n), BF1...]
    another operation x29 -> x0, matrix products: 64.1 us -> none  [the longest x15 40.8 us: shards(): lax.linalg.triangular_solve(lower, cross, left_side=False, lower=True, tr...]
    psum x5 -> x1, blocking collectives: 122 us -> 77.6 us  [shards(): stats = lax.psum(stats[:2], GRP_DEV) / total_rows]
    another operation x33 -> x0, local copies, waits for them, and re-layouts: 24.9 us -> none
    dot_general x2 -> x0, matrix products: 9.96 us -> none  [kernel_block(): inner = jnp.dot(left, right.T, preferred_element_type=jnp.float32)]
    convert_element_type x1 -> x0, local copies, waits for them, and re-layouts: 6.39 us -> none  [shards(): return (centered / jnp.sqrt(var + 1e-05)[None, :]).astype(jnp.bfloat16)]
  transfers between devices with their start and end apart: 0 -> 1, of which waited for: 0 -> 1; matrix products, arithmetic and copies ran while one was open for 0% -> 0% of each run, Pallas kernels for 0% -> 0%
where the time goes in v1:
time: 440 us
  waiting for transfers between devices  258 us (59%)
  blocking collectives  77.6 us (18%)
  Pallas kernels  69.8 us (16%)
  between operations  13.4 us (3%)
  local copies, waits for them, and re-layouts  12 us (3%)
  other arithmetic  9.09 us (2%)
    psum x1, waiting for transfers between devices, shards(): marks = lax.psum(filled, GRP_DEV)  258 us
    psum x1, blocking collectives, shards(): stats = lax.psum(stats[:2], GRP_DEV) / total_rows  77.6 us
    pallas_call x1, Pallas kernels, factor(): pl.pallas_call(factor_kernel, out_shape=[jax.ShapeDtypeStruct((n, n), BF1...  54.9 us
    pallas_call x1, Pallas kernels, raw_features(): pl.pallas_call(raw_kernel, grid=(rows // ROWS_STEP,), out_shape=[jax.Shap...  15 us
  transfers between devices with their start and end apart: 1, of which 1 were waited for; matrix products, arithmetic and copies ran while one was open for 0% of the time, Pallas kernels for 0%

profile of v1, /device:TPU:1, one launch (start us, length us, event | category | flops | bytes accessed | tf_op | source)
XLA Modules:
  0.0 439.9 jit_solution(13450198175049212821)
XLA Ops:
  6.5 0.0 all-reduce.2.cloned.1.call-start
  6.5 0.7 compare_and_fusion
  7.2 0.7 fusion
  7.9 4.8 %gather_fusion = bf16[1024,256]{1,0:T(8,128)(2,1)S(1)} fusion(bf16[2048,256]{1,0:T(8,128)(2,1)} %points_ref.1, s32[1024]{0:T(1024)S(1)} %fusion), kind=kCustom, calls=%fused_computation | custom fusion | bytes 1052672 | tf_op jit(solution)/shard_map/gather | solution.py:187
  12.8 1.0 broadcast_select_fusion
  13.8 0.0 all-reduce.2.cloned.1.call-update
  13.8 257.9 %all-reduce.2.cloned.1.call-done.marks_ref = bf16[1024,256]{1,0:T(8,128)(2,1)} async-done(((bf16[1024,256]{1,0:T(8,128)(2,1)}), bf16[1024,256]{1,0:T(8,128)(2,1)}) %all-reduce.2.cloned.1.call-update) | async-done | bytes 524304 | tf_op jit(solution)/shard_map/psum | solution.py:189
  271.7 0.0 copy-start.2
  271.7 1.0 copy-done.2
  272.7 0.0 copy-start.4
  272.7 0.7 copy-done.4
  273.4 54.9 %factor.1 = (bf16[1024,1024]{1,0:T(8,128)(2,1)S(1)}, bf16[1024,1024]{1,0:T(8,128)(2,1)S(1)}, f32[8,1024]{1,0:T(8,128)S(1)}) custom-call(bf16[1024,256]{1,0:T(8,128)(2,1)S(1)} %copy-done.2, f32[1,1024]{1,0:T(1,128)S(1)} %bitcast.3), custom_call_target="tpu_custom_call" | custom-call | tf_op jit(solution)/shard_map/factor/pallas_call | solution.py:117
  328.3 0.0 copy-start
  328.3 1.2 copy-done
  329.5 0.0 copy-start.3
  329.5 1.0 copy-done.3
  330.5 15.0 %raw.1 = (f32[2048,1024]{1,0:T(8,128)S(1)}, f32[8,1024]{1,0:T(8,128)S(1)}) custom-call(bf16[2048,256]{1,0:T(8,128)(2,1)S(1)} %copy-done, bf16[1024,256]{1,0:T(8,128)(2,1)S(1)} %copy-done.3, f32[8,1024]{1,0:T(8,128)S(1)} %get-tuple-element.10.norm_ref, bf16[1024,1024]{1,0:T(8,128)(2,1)S(1)} %get-tuple-element.11.hi_ref, ...), custom_call_target="tpu_custom_call" | custom-call | tf_op jit(solution)/shard_map/raw/pallas_call | solution.py:162
  345.5 0.0 copy-start.1
  345.5 3.2 copy-done.1
  348.7 77.6 %psum.15 = f32[2,1024]{1,0:T(2,128)S(1)} all-reduce(f32[2,1024]{1,0:T(2,128)S(1)} %slice.10), channel_id=1, replica_groups=mesh['grp'=4,'dev_0'=4,'dev_1'=8,'dev_2'=2] {'grp','dev_0','dev_1','dev_2'}, use_global_device_ids=true, to_apply=%region_1.2 | all-reduce | flops 2048 | bytes 16384 | tf_op jit(solution)/shard_map/psum | solution.py:193
  426.4 6.7 %multiply_convert_fusion = bf16[2048,1024]{1,0:T(8,128)(2,1)} fusion(f32[2048,1024]{1,0:T(8,128)} %copy-done.1, f32[1024]{0:T(1024)S(1)} %bitcast.5, f32[1024]{0:T(1024)S(1)} %bitcast.4), kind=kLoop, calls=%fused_computation.1 | loop fusion | flops 6291456 | bytes 12591104 | tf_op jit(solution)/shard_map/convert_element_type | solution.py:195
  (3 shorter events, 0.0 us)
Async XLA Ops:
  6.5 265.1 %all-reduce.2.cloned.1.call-start = ((), (), s32[]{:S(2)}) async-start(), calls=%async_computation | async-start | bytes 1048576 | tf_op jit(solution)/shard_map/psum | solution.py:189
  271.7 1.0 copy-start.2
  272.7 0.7 copy-start.4
  328.3 1.2 copy-start
  329.5 1.0 copy-start.3
  345.5 3.2 copy-start.1
Sparse Core Ops, SparseCore 0:
  13.9 257.7 all-reduce.1

commit v2 on v1

--- a/solution.py
+++ b/solution.py
@@ -151,8 +151,11 @@
         x += mul(cl[:, :k], hi_ref[cols, :k])
         x += mul(ch[:, :k], lo_ref[cols, :k])
         raw_ref[:, cols] = x
-        stats_ref[0:1, cols] += jnp.sum(x, axis=0, keepdims=True)
-        stats_ref[1:2, cols] += jnp.sum(jnp.square(x), axis=0, keepdims=True)
+        for i in range(2):
+            y = x[:, i * 128 : (i + 1) * 128]
+            r = 2 * j + i
+            stats_ref[r : r + 1, :] += jnp.sum(y, axis=0, keepdims=True)
+            stats_ref[8 + r : 9 + r, :] += jnp.sum(jnp.square(y), axis=0, keepdims=True)
 
 
 def raw_features(points, marks, norms, hi, lo):
@@ -162,7 +165,7 @@
     return pl.pallas_call(
         raw_kernel,
         grid=(rows // ROWS_STEP,),
-        out_shape=[jax.ShapeDtypeStruct((rows, n), F32), jax.ShapeDtypeStruct((8, n), F32)],
+        out_shape=[jax.ShapeDtypeStruct((rows, n), F32), jax.ShapeDtypeStruct((16, n // 8), F32)],
         in_specs=[
             pl.BlockSpec((ROWS_STEP, d), lambda i: (i, 0)),
             whole((n, d)),
@@ -172,27 +175,266 @@
         ],
         out_specs=[
             pl.BlockSpec((ROWS_STEP, n), lambda i: (i, 0)),
-            pl.BlockSpec((8, n), lambda i: (0, 0)),
+            pl.BlockSpec((16, n // 8), lambda i: (0, 0)),
         ],
         name="raw",
         compiler_params=pltpu.CompilerParams(vmem_limit_bytes=40 << 20),
     )(points, marks, norms, hi, lo)
 
 
+MESH_IDS = pl.DeviceIdType.MESH
+SLOTS = 16
+WINDOW = 128
+DMA = pltpu.SemaphoreType.DMA
+
+
+def position():
+    inner = lax.axis_index("dev_1") * 2 + lax.axis_index("dev_2")
+    outer = lax.axis_index("grp") * 4 + lax.axis_index("dev_0")
+    return inner, outer
+
+
+def inner_peer(i):
+    return {"dev_1": lax.div(i, 2), "dev_2": lax.rem(i, 2)}
+
+
+def outer_peer(o):
+    return {"grp": lax.div(o, 4), "dev_0": lax.rem(o, 4)}
+
+
+def others(me, body):
+    def step(k, carry):
+        body(k, lax.rem(me + k, 16), lax.rem(me + 16 - k, 16))
+        return carry
+
+    lax.fori_loop(1, 16, step, 0)
+
+
+def greet(inner, outer):
+    barrier = pltpu.get_barrier_semaphore()
+
+    def inner_step(k, to, frm):
+        pl.semaphore_signal(barrier, inc=1, device_id=inner_peer(to), device_id_type=MESH_IDS)
+
+    def outer_step(k, to, frm):
+        pl.semaphore_signal(barrier, inc=1, device_id=outer_peer(to), device_id_type=MESH_IDS)
+
+    others(inner, inner_step)
+    others(outer, outer_step)
+    return barrier
+
+
+def send(src, dst, send_sem, recv_sem, peer):
+    return pltpu.make_async_remote_copy(
+        src_ref=src, dst_ref=dst, send_sem=send_sem, recv_sem=recv_sem, device_id=peer, device_id_type=MESH_IDS
+    )
+
+
+def gather_kernel(sel_ref, place_ref, points_ref, out_ref, rows, line, window, s1, r1, s2, r2, s3, r3):
+    inner, outer = position()
+    core = lax.rem(inner, 2)
+    barrier = greet(inner, outer)
+    d = points_ref.shape[1]
+    count = points_ref.shape[0]
+    pick = (lax.broadcasted_iota(jnp.int32, (SLOTS, count), 1) == sel_ref[...]).astype(BF16)
+    picked = jnp.dot(pick, points_ref[...], preferred_element_type=F32).astype(BF16)
+    rows[...] = picked
+    line[inner] = picked
+    pl.semaphore_wait(barrier, 30)
+
+    def first(k, to, frm):
+        send(rows, line.at[inner], s1.at[k], r1.at[inner], inner_peer(to)).start()
+
+    others(inner, first)
+
+    def first_done(k, to, frm):
+        send(rows, line.at[frm], s1.at[k], r1.at[frm], inner_peer(to)).wait()
+
+    others(inner, first_done)
+    pick = (
+        lax.broadcasted_iota(jnp.int32, (WINDOW, 16 * SLOTS), 0) == place_ref[...]
+    ).astype(BF16)
+    compact = jnp.dot(pick, line[...].reshape(16 * SLOTS, d), preferred_element_type=F32).astype(BF16)
+    window[...] = compact
+    out_ref[outer] = compact
+    half = pl.ds(pl.multiple_of(core * (WINDOW // 2), WINDOW // 2), WINDOW // 2)
+    rest = pl.ds(pl.multiple_of((1 - core) * (WINDOW // 2), WINDOW // 2), WINDOW // 2)
+
+    def second(k, to, frm):
+        send(window.at[half], out_ref.at[outer, half], s2.at[k], r2.at[outer], outer_peer(to)).start()
+
+    others(outer, second)
+    partner = {"dev_2": 1 - core}
+
+    def forward(k, to, frm):
+        send(window.at[half], out_ref.at[frm, half], s2.at[k], r2.at[frm], outer_peer(to)).wait_recv()
+        send(out_ref.at[frm, half], out_ref.at[frm, half], s3.at[k], r3.at[frm], partner).start()
+
+    others(outer, forward)
+
+    def last(k, to, frm):
+        send(window.at[half], out_ref.at[frm, half], s2.at[k], r2.at[frm], outer_peer(to)).wait_send()
+        copy = send(out_ref.at[frm, rest], out_ref.at[frm, rest], s3.at[k], r3.at[frm], partner)
+        copy.wait_send()
+        copy.wait_recv()
+
+    others(outer, last)
+
+
+def gather_windows(sel, place, points):
+    d = points.shape[1]
+    return pl.pallas_call(
+        gather_kernel,
+        out_shape=jax.ShapeDtypeStruct((16, WINDOW, d), BF16),
+        in_specs=[VMEM, VMEM, VMEM],
+        out_specs=VMEM,
+        scratch_shapes=[
+            pltpu.VMEM((SLOTS, d), BF16),
+            pltpu.VMEM((16, SLOTS, d), BF16),
+            pltpu.VMEM((WINDOW, d), BF16),
+        ]
+        + [DMA((16,))] * 6,
+        name="gather",
+        compiler_params=pltpu.CompilerParams(collective_id=0, has_side_effects=True),
+    )(sel, place, points)
+
+
+def place_kernel(first_ref, windows_ref, before_ref, marks_ref, held):
+    n, d = marks_ref.shape
+    held[:n, :] = before_ref[...].astype(F32)
+    for g in range(16):
+        lo = first_ref[g]
+
+        @pl.when(first_ref[g + 1] > lo)
+        def _():
+            base = pl.multiple_of(lax.div(lo, 8) * 8, 8)
+            block = jnp.concatenate([windows_ref[g].astype(F32), jnp.zeros((8, d), F32)], 0)
+            moved = pltpu.roll(block, lo - base, 0)
+            old = held[pl.ds(base, 8), :]
+            at = lax.broadcasted_iota(jnp.int32, (8, d), 0)
+            held[pl.ds(base, 8), :] = jnp.where(at >= lo - base, moved[:8], old)
+            held[pl.ds(base + 8, WINDOW), :] = moved[8:]
+
+    marks_ref[...] = held[:n, :].astype(BF16)
+
+
+def place_windows(first, windows, before):
+    n, d = before.shape
+    return pl.pallas_call(
+        place_kernel,
+        out_shape=jax.ShapeDtypeStruct((n, d), BF16),
+        in_specs=[pl.BlockSpec(memory_space=pltpu.SMEM), VMEM, VMEM],
+        out_specs=VMEM,
+        scratch_shapes=[pltpu.VMEM((n + WINDOW + 8, d), F32)],
+        name="place",
+    )(first, windows, before)
+
+
+def gather_marks(points, ids):
+    count, d = points.shape
+    n = ids.shape[0]
+    devices = lax.axis_size(GRP_DEV)
+    me = lax.axis_index(GRP_DEV)
+    bounds = jnp.sum(
+        (ids[None, :] < (jnp.arange(devices + 1, dtype=jnp.int32) * count)[:, None]).astype(jnp.int32), axis=1
+    )
+    lines = bounds[::16]
+    fits = (jnp.max(bounds[1:] - bounds[:-1]) <= SLOTS) & (jnp.max(lines[1:] - lines[:-1]) <= WINDOW)
+    step = jnp.where(fits, n, SLOTS)
+    padded = jnp.concatenate([ids, jnp.zeros((SLOTS,), jnp.int32)])
+    slot = jnp.arange(SLOTS, dtype=jnp.int32)
+
+    def turn(start, before):
+        b = jnp.clip(bounds, start, start + step)
+        mine = lax.dynamic_slice(b, (me,), (2,))
+        local = lax.dynamic_slice(padded, (mine[0],), (SLOTS,)) - me * count
+        sel = jnp.where(mine[0] + slot < mine[1], local, -1)
+        line = lax.dynamic_slice(b, (me // 16 * 16,), (17,))
+        place = line[:16, None] + slot[None, :]
+        place = jnp.where(place < line[1:, None], place - line[0], -1)
+        return place_windows(b[::16], gather_windows(sel.reshape(SLOTS, 1), place.reshape(1, 16 * SLOTS), points), before)
+
+    marks = turn(jnp.int32(0), jnp.zeros((n, d), BF16))
+    return lax.while_loop(
+        lambda c: c[0] < n, lambda c: (c[0] + step, turn(c[0], c[1])), (step, marks)
+    )[1]
+
+
+def stats_kernel(rows_total, stats_ref, out_ref, mid, line, cross, s1, r1, s2, r2):
+    inner, outer = position()
+    barrier = greet(inner, outer)
+    line[inner] = stats_ref[...]
+    pl.semaphore_wait(barrier, 30)
+
+    def first(k, to, frm):
+        send(stats_ref, line.at[inner], s1.at[k], r1.at[inner], inner_peer(to)).start()
+
+    def first_done(k, to, frm):
+        send(stats_ref, line.at[frm], s1.at[k], r1.at[frm], inner_peer(to)).wait()
+
+    others(inner, first)
+    others(inner, first_done)
+    total = jnp.sum(line[...], axis=0)
+    mid[...] = total
+    cross[outer] = total
+
+    def second(k, to, frm):
+        send(mid, cross.at[outer], s2.at[k], r2.at[outer], outer_peer(to)).start()
+
+    def second_done(k, to, frm):
+        send(mid, cross.at[frm], s2.at[k], r2.at[frm], outer_peer(to)).wait()
+
+    others(outer, second)
+    others(outer, second_done)
+    total = jnp.sum(cross[...], axis=0) / rows_total
+    mean = total[:8]
+    out_ref[:8] = mean
+    out_ref[8:] = lax.rsqrt(jnp.maximum(total[8:] - jnp.square(mean), 0.0) + 1e-05)
+
+
+def mean_and_scale(stats, rows_total):
+    shape = stats.shape
+    return pl.pallas_call(
+        functools.partial(stats_kernel, rows_total),
+        out_shape=jax.ShapeDtypeStruct(shape, F32),
+        in_specs=[VMEM],
+        out_specs=VMEM,
+        scratch_shapes=[
+            pltpu.VMEM(shape, F32),
+            pltpu.VMEM((16,) + shape, F32),
+            pltpu.VMEM((16,) + shape, F32),
+        ]
+        + [DMA((16,))] * 4,
+        name="stats",
+        compiler_params=pltpu.CompilerParams(collective_id=1, has_side_effects=True),
+    )(stats)
+
+
+def standardize_kernel(raw_ref, stats_ref, out_ref):
+    for i in range(8):
+        cols = slice(i * 128, (i + 1) * 128)
+        x = raw_ref[:, cols] - stats_ref[i : i + 1, :]
+        out_ref[:, cols] = (x * stats_ref[8 + i : 9 + i, :]).astype(BF16)
+
+
+def standardize(raw, stats):
+    rows, n = raw.shape
+    block = pl.BlockSpec((ROWS_STEP, n), lambda i: (i, 0))
+    return pl.pallas_call(
+        standardize_kernel,
+        grid=(rows // ROWS_STEP,),
+        out_shape=jax.ShapeDtypeStruct((rows, n), BF16),
+        in_specs=[block, pl.BlockSpec(stats.shape, lambda i: (0, 0))],
+        out_specs=block,
+        name="standardize",
+    )(raw, stats)
+
+
 def shards(points, ridge, landmark_ids):
-    count = points.shape[0]
-    start = lax.axis_index(GRP_DEV) * count
-    offset = landmark_ids - start
-    inside = (offset >= 0) & (offset < count)
-    picked = points[jnp.clip(offset, 0, count - 1)]
-    filled = jnp.where(inside[:, None], picked, jnp.zeros((), BF16))
-    marks = lax.psum(filled, GRP_DEV)
+    marks = gather_marks(points, landmark_ids)
     hi, lo, norms = factor(marks, ridge)
     raw, stats = raw_features(points, marks, norms, hi, lo)
-    total_rows = count * lax.axis_size(GRP_DEV)
-    stats = lax.psum(stats[:2], GRP_DEV) / total_rows
-    mean, var = stats[0], jnp.maximum(stats[1] - jnp.square(stats[0]), 0.0)
-    return ((raw - mean[None, :]) * lax.rsqrt(var + 1e-05)[None, :]).astype(BF16)
+    return standardize(raw, mean_and_scale(stats, points.shape[0] * lax.axis_size(GRP_DEV)))
 
 
 def solution(mesh):

time: 440 us -> 144 us (0.33)
  waiting for transfers between devices: 258 us -> 0 us
  blocking collectives: 77.6 us -> 0 us
  Pallas kernels: 69.8 us -> 127 us
  between operations: 13.4 us -> 3.27 us
  other arithmetic: 9.09 us -> 4.53 us
    psum x1 -> x0, waiting for transfers between devices: 258 us -> none  [shards(): marks = lax.psum(filled, GRP_DEV)]
    psum x1 -> x0, blocking collectives: 77.6 us -> none  [shards(): stats = lax.psum(stats[:2], GRP_DEV) / total_rows]
    pallas_call x0 -> x4, Pallas kernels: none -> 57 us  [the longest x1 29.3 us: gather_windows(): pl.pallas_call(gather_kernel, out_shape=jax.ShapeDtypeStruct((16, WINDOW,...]
    convert_element_type x1 -> x0, other arithmetic: 6.68 us -> none  [shards(): ((raw - mean[None, :]) * lax.rsqrt(var + 1e-05)[None, :]).astype(BF16)]
    gather x1 -> x0, local copies, waits for them, and re-layouts: 4.82 us -> none  [shards(): picked = points[jnp.clip(offset, 0, count - 1)]]
  transfers between devices with their start and end apart: 1 -> 0, of which waited for: 1 -> 0; matrix products, arithmetic and copies ran while one was open for 0% -> 0% of each run, Pallas kernels for 0% -> 0%
where the time goes in v2:
time: 144 us
  Pallas kernels  127 us (88%)
  local copies, waits for them, and re-layouts  8.83 us (6%)
  other arithmetic  4.53 us (3%)
  between operations  3.27 us (2%)
    pallas_call x1, Pallas kernels, factor(): pl.pallas_call(factor_kernel, out_shape=[jax.ShapeDtypeStruct((n, n), BF1...  54.8 us
    pallas_call x1, Pallas kernels, gather_windows(): pl.pallas_call(gather_kernel, out_shape=jax.ShapeDtypeStruct((16, WINDOW,...  29.3 us
    pallas_call x1, Pallas kernels, mean_and_scale(): pl.pallas_call(functools.partial(stats_kernel, rows_total), out_shape=jax...  17.4 us
    pallas_call x1, Pallas kernels, raw_features(): pl.pallas_call(raw_kernel, grid=(rows // ROWS_STEP,), out_shape=[jax.Shap...  15 us
    pallas_call x1, Pallas kernels, standardize(): pl.pallas_call(standardize_kernel, grid=(rows // ROWS_STEP,), out_shape=j...  8.03 us
    unnamed x8, local copies, waits for them, and re-layouts  4.48 us

profile of v2, /device:TPU:1, one launch (start us, length us, event | category | flops | bytes accessed | tf_op | source)
XLA Modules:
  0.0 143.5 jit_solution(15249998173409840661)
XLA Ops:
  0.0 1.0 convert_reduce_fusion
  1.0 0.7 subtract_reduce_fusion
  2.3 0.1 slice.70
  2.4 0.7 subtract_reduce_fusion.1
  3.8 0.1 dynamic_slice.29
  3.9 0.1 dynamic_slice.27
  4.0 0.6 slice.73.first_ref
  4.6 0.6 fusion.11
  7.0 2.0 %fusion.7 = s32[16,1]{0,1:T(1,128)S(1)} fusion(s32[]{:T(128)S(6)} %select_n.79, s32[1024]{0:T(1024)} %param.7, s32[]{:T(128)} %mul.36, s32[]{:T(128)} %bitcast.1, s32[]{:T(128)} %bitcast), kind=kLoop, calls=%fused_computation.18 | loop fusion | flops 64 | bytes 4176 | tf_op jit(solution)/shard_map/reshape | solution.py:355
  9.0 0.1 fusion.10
  9.1 0.1 subtract_select_fusion
  9.2 0.7 select_n.84.place_ref
  9.9 0.7 copy.7.sel_ref
  10.6 0.7 concatenate.3
  11.2 0.0 copy-start.3
  11.2 29.3 %gather.2.windows_ref = bf16[16,128,256]{2,1,0:T(8,128)(2,1)} custom-call(s32[16,1]{1,0:T(8,128)} %copy.7.sel_ref, s32[1,256]{1,0:T(1,128)} %select_n.84.place_ref, bf16[2048,256]{1,0:T(8,128)(2,1)} %points_ref.3), custom_call_target="tpu_custom_call" | custom-call | tf_op jit(solution)/shard_map/gather/pallas_call | solution.py:286
  40.5 0.8 broadcast_in_dim.32.before_ref
  41.4 2.3 %place.5 = bf16[1024,256]{1,0:T(8,128)(2,1)S(1)} custom-call(s32[17]{0:T(128)} %slice.73.first_ref, bf16[16,128,256]{2,1,0:T(8,128)(2,1)} %gather.2.windows_ref, bf16[1024,256]{1,0:T(8,128)(2,1)} %broadcast_in_dim.32.before_ref), custom_call_target="tpu_custom_call" | custom-call | tf_op jit(solution)/shard_map/place/pallas_call | solution.py:323
  43.7 0.0 copy-done.3
  43.7 0.0 copy-start.2
  43.7 0.7 copy-done.2
  44.4 54.8 %factor.1 = (bf16[1024,1024]{1,0:T(8,128)(2,1)S(1)}, bf16[1024,1024]{1,0:T(8,128)(2,1)S(1)}, f32[8,1024]{1,0:T(8,128)S(1)}) custom-call(bf16[1024,256]{1,0:T(8,128)(2,1)S(1)} %get-tuple-element.211.marks_ref, f32[1,1024]{1,0:T(1,128)S(1)} %bitcast.23), custom_call_target="tpu_custom_call" | custom-call | tf_op jit(solution)/shard_map/factor/pallas_call | solution.py:117
  99.2 15.0 %raw.1 = (f32[2048,1024]{1,0:T(8,128)S(1)}, f32[16,128]{1,0:T(8,128)S(1)}) custom-call(bf16[2048,256]{1,0:T(8,128)(2,1)S(1)} %get-tuple-element.383, bf16[1024,256]{1,0:T(8,128)(2,1)S(1)} %get-tuple-element.211.marks_ref, f32[8,1024]{1,0:T(8,128)S(1)} %get-tuple-element.212.norm_ref, bf16[1024,1024]{1,0:T(8,128)(2,1)S(1)} %get-tuple-element.213.hi_ref, ...), custom_call_target="tpu_custom_call" | custom-call | tf_op jit(solution)/shard_map/raw/pallas_call | solution.py:165
  114.3 0.0 copy-start
  114.3 3.2 %copy-done = f32[2048,1024]{1,0:T(8,128)} copy-done((f32[2048,1024]{1,0:T(8,128)}, f32[2048,1024]{1,0:T(8,128)S(1)}, u32[]{:S(2)}) %copy-start) | copy-done | bytes 8388632
  117.5 0.0 copy-start.1
  117.5 0.6 copy-done.1
  118.1 17.4 %stats.1.stats_ref = f32[16,128]{1,0:T(8,128)} custom-call(f32[16,128]{1,0:T(8,128)} %copy-done.1), custom_call_target="tpu_custom_call" | custom-call | tf_op jit(solution)/shard_map/stats/pallas_call | solution.py:397
  135.5 8.0 %standardize.1 = bf16[2048,1024]{1,0:T(8,128)(2,1)} custom-call(f32[2048,1024]{1,0:T(8,128)} %copy-done, f32[16,128]{1,0:T(8,128)} %stats.1.stats_ref), custom_call_target="tpu_custom_call" | custom-call | tf_op jit(solution)/shard_map/standardize/pallas_call | solution.py:423
  (3 shorter events, 0.0 us)
Async XLA Ops:
  11.2 32.4 %copy-start.3 = (bf16[2048,256]{1,0:T(8,128)(2,1)S(1)}, bf16[2048,256]{1,0:T(8,128)(2,1)}, u32[]{:S(2)}) copy-start(bf16[2048,256]{1,0:T(8,128)(2,1)} %points_ref.3) | copy-start | bytes 3145732
  43.7 0.7 copy-start.2
  114.3 3.2 %copy-start = (f32[2048,1024]{1,0:T(8,128)}, f32[2048,1024]{1,0:T(8,128)S(1)}, u32[]{:S(2)}) copy-start(f32[2048,1024]{1,0:T(8,128)S(1)} %get-tuple-element.215.raw_ref) | copy-start | bytes 25165828
  117.5 0.6 copy-start.1

commit v3 on v2

v3 whole, which is shorter than its diff:
```python
import functools

import jax
import jax.numpy as jnp
from jax import lax
from jax.experimental import pallas as pl
from jax.experimental.pallas import tpu as pltpu
from jax.sharding import Mesh
from jax.sharding import PartitionSpec as P

GRP_DEV = ("grp", "dev_0", "dev_1", "dev_2")
F32 = jnp.float32
BF16 = jnp.bfloat16
HI = lax.Precision.HIGHEST
BLK = 128
ROWS_STEP = 256
VMEM = pl.BlockSpec(memory_space=pltpu.VMEM)


def lane(x, c):
    return jnp.broadcast_to(x[:, c : c + 1], (8, 128))


def sub(x, k):
    return jnp.broadcast_to(x[k : k + 1, :], (8, 128))


def eliminate64(g1, g2, lane0):
    row = lax.broadcasted_iota(jnp.int32, (8, 128), 0)
    for q in range(8):
        b = [[lane(g1[t], lane0 + 8 * q + c) for t in range(q, 8)] for c in range(8)]
        root = None
        scale, inverse, last_scale, last_inverse = None, None, None, None
        for k in range(8):
            p = sub(b[k][0], k)
            r = 1.0 / p
            rs = lax.rsqrt(p if k == 0 else p * inverse)
            root = rs if k == 0 else jnp.where(row == k, rs, root)
            m = [x * r for x in b[k]]
            m[0] = jnp.where(row > k, m[0], 0.0)
            if k < 7:
                pc, bk = p, b[k]
                if last_inverse is not None:
                    pc, bk = p * last_inverse, [x * last_inverse for x in b[k]]
                for c in range(k + 1, 8):
                    a = sub(b[c][0], k)
                    b[c] = [pc * x - y * a for x, y in zip(b[c], bk)]
                if k == 0:
                    scale, inverse = p, r
                else:
                    next_inverse = inverse * r if last_scale is None else inverse * r * last_scale
                    scale, last_scale = scale * pc, scale
                    inverse, last_inverse = next_inverse, inverse
            a1 = sub(g1[q], k)
            a2 = sub(g2[q], k)
            for t in range(q, 8):
                g1[t] = g1[t] - m[t - q] * a1
                g2[t] = g2[t] - m[t - q] * a2
        g1[q] = g1[q] * root
        g2[q] = g2[q] * root
    return g1, g2


def split(x):
    high = x.astype(BF16)
    return high, (x - high.astype(F32)).astype(BF16)


def cat(xs, axis):
    return jnp.concatenate(xs, axis)


def pair_dot(a, high, low):
    return jnp.dot(a, high, preferred_element_type=F32) + jnp.dot(a, low, preferred_element_type=F32)


def inverse_factor(s, eye):
    rows = lambda x: [x[8 * t : 8 * t + 8] for t in range(8)]
    u, v = eliminate64(rows(s[:64]), rows(eye[:64]), 0)
    v = cat(v, 0)
    high, low = split(cat([cat(u, 0), v], 1))
    uh, ul = high[:, :BLK], low[:, :BLK]
    t = lax.dot_general(
        cat([uh, ul, uh, ul], 0),
        cat([high, high, low, low], 0),
        (((0,), (0,)), ((), ())),
        preferred_element_type=F32,
    )[64:]
    _, v2 = eliminate64(rows(s[64:] - t[:, :BLK]), rows(eye[64:] - t[:, BLK:]), 64)
    return cat([v] + v2, 0)


def factor_kernel(marks_ref, ridge_ref, hi_ref, lo_ref, norm_ref, m, rt, rh, rl):
    n, d = marks_ref.shape
    nb = n // BLK
    eye = (
        lax.broadcasted_iota(jnp.int32, (BLK, BLK), 0)
        == lax.broadcasted_iota(jnp.int32, (BLK, BLK), 1)
    ).astype(F32)
    sq = jnp.square(marks_ref[...].astype(F32))
    nr = lax.dot_general(
        jnp.ones((8, d), F32), sq, (((1,), (1,)), ((), ())), preferred_element_type=F32, precision=HI
    )
    norm_ref[...] = nr
    for i in range(nb):
        rows = slice(i * BLK, (i + 1) * BLK)
        blk = marks_ref[rows, :]
        nc = jnp.sum(jnp.square(blk.astype(F32)), axis=1, keepdims=True)
        g = lax.dot_general(blk, marks_ref[...], (((1,), (1,)), ((), ())), preferred_element_type=F32)
        m[rows, :] = jnp.exp((2.0 * g - nc - nr[:1]) * (1.0 / (2.0 * d)))
        m[rows, rows] += eye * ridge_ref[:, rows]
    rt[...] = jnp.zeros_like(rt)
    rh[...] = jnp.zeros_like(rh)
    rl[...] = jnp.zeros_like(rl)

    def step(j, carry):
        here = pl.ds(pl.multiple_of(j * BLK, BLK), BLK)
        linv = inverse_factor(m[here, here], eye)
        for i in range(1, nb):
            rows = slice(i * BLK, (i + 1) * BLK)
            m[rows, :] = m[rows, :] - pair_dot(rt[rows, :], rh[...], rl[...])
        m[here, here] = eye
        high, low = split(m[here, :])
        r = pair_dot(cat(split(linv), 1), cat([high, high], 0), cat([low, low], 0))
        m[here, :] = r
        high, low = split(r)
        rh[:BLK, :] = high
        rh[BLK:, :] = high
        rl[:BLK, :] = low
        rl[BLK:, :] = low
        for i in range(1, nb):
            rows = slice(i * BLK, (i + 1) * BLK)
            m[rows, here] = jnp.where(i > j, 0.0, m[rows, here])
            high, low = split(jnp.where(i > j + 1, r[:, rows].T, 0.0))
            rt[rows, :BLK] = high
            rt[rows, BLK:] = low
        after = pl.ds(pl.multiple_of(jnp.minimum(j + 1, nb - 1) * BLK, BLK), BLK)
        t = jnp.where(j + 1 < nb, m[here, after].T, 0.0)
        m[after, :] = m[after, :] - pair_dot(cat(split(t), 1), rh[...], rl[...])
        return carry

    lax.fori_loop(0, nb, step, 0)
    for i in range(nb):
        rows = slice(i * BLK, (i + 1) * BLK)
        x = m[rows, :]
        x = jnp.where(lax.broadcasted_iota(jnp.int32, x.shape, 1) < (i + 1) * BLK, x, 0.0)
        hi_ref[rows, :], lo_ref[rows, :] = split(x)


def factor(marks, ridge):
    n = marks.shape[0]
    return pl.pallas_call(
        factor_kernel,
        out_shape=[
            jax.ShapeDtypeStruct((n, n), BF16),
            jax.ShapeDtypeStruct((n, n), BF16),
            jax.ShapeDtypeStruct((8, n), F32),
        ],
        in_specs=[VMEM, VMEM],
        out_specs=[VMEM, VMEM, VMEM],
        scratch_shapes=[
            pltpu.VMEM((n, n), F32),
            pltpu.VMEM((n, 2 * BLK), BF16),
            pltpu.VMEM((2 * BLK, n), BF16),
            pltpu.VMEM((2 * BLK, n), BF16),
        ],
        name="factor",
        compiler_params=pltpu.CompilerParams(vmem_limit_bytes=40 << 20),
    )(marks, ridge.reshape(1, n))


MESH_IDS = pl.DeviceIdType.MESH
SLOTS = 16
WINDOW = 128
DMA = pltpu.SemaphoreType.DMA


def position():
    inner = lax.axis_index("dev_1") * 2 + lax.axis_index("dev_2")
    outer = lax.axis_index("grp") * 4 + lax.axis_index("dev_0")
    return inner, outer


def inner_peer(i):
    return {"dev_1": lax.div(i, 2), "dev_2": lax.rem(i, 2)}


def outer_peer(o):
    return {"grp": lax.div(o, 4), "dev_0": lax.rem(o, 4)}


def others(me, body):
    def step(k, carry):
        body(k, lax.rem(me + k, 16), lax.rem(me + 16 - k, 16))
        return carry

    lax.fori_loop(1, 16, step, 0)


def greet(inner, outer):
    barrier = pltpu.get_barrier_semaphore()

    def inner_step(k, to, frm):
        pl.semaphore_signal(barrier, inc=1, device_id=inner_peer(to), device_id_type=MESH_IDS)

    def outer_step(k, to, frm):
        pl.semaphore_signal(barrier, inc=1, device_id=outer_peer(to), device_id_type=MESH_IDS)

    others(inner, inner_step)
    others(outer, outer_step)
    return barrier


def send(src, dst, send_sem, recv_sem, peer):
    return pltpu.make_async_remote_copy(
        src_ref=src, dst_ref=dst, send_sem=send_sem, recv_sem=recv_sem, device_id=peer, device_id_type=MESH_IDS
    )


def count_below(ids, starts):
    return jnp.sum((ids < starts).astype(F32), axis=1, keepdims=True).astype(jnp.int32)


def gather_kernel(
    ids_ref, turn_ref, points_ref, marks_ref, over_ref, rows, line, window, windows, s1, r1, s2, r2, s3, r3
):
    inner, outer = position()
    core = lax.rem(inner, 2)
    barrier = greet(inner, outer)
    count, d = points_ref.shape
    n = marks_ref.shape[0]
    iota = lambda shape, axis: lax.broadcasted_iota(jnp.int32, shape, axis)
    ids = ids_ref[...]
    low, high = turn_ref[0:1, 0:1], turn_ref[1:2, 0:1]
    clip = lambda x: jnp.minimum(jnp.maximum(x, low), high)
    start = (outer * 16 + inner) * count
    first = clip(count_below(ids, jnp.full((1, n), start)))
    mark = iota((SLOTS, n), 1)
    wanted = (
        (mark - first == iota((SLOTS, n), 0)) & (ids >= start) & (ids < start + count) & (mark < high)
    )
    sel = jnp.sum(jnp.where(wanted, ids - start + 1, 0).astype(F32), axis=1, keepdims=True) - 1.0
    pick = (iota((SLOTS, count), 1).astype(F32) == sel).astype(BF16)
    picked = jnp.dot(pick, points_ref[...], preferred_element_type=F32).astype(BF16)
    rows[...] = picked
    line[inner] = picked
    at = clip(count_below(ids, (outer * 16 + iota((24, n), 0)) * count))
    slot = iota((1, 16 * SLOTS), 1)
    place, limit = slot, slot
    for i in range(16):
        own = (slot >= i * SLOTS) & (slot < (i + 1) * SLOTS)
        place = jnp.where(own, at[i : i + 1] + (slot - i * SLOTS), place)
        limit = jnp.where(own, at[i + 1 : i + 2], limit)
    place = jnp.where(place < limit, place - at[0:1], -1)
    pick = (iota((WINDOW, 16 * SLOTS), 0) == place).astype(BF16)
    lines = count_below(ids, iota((24, n), 0) * (16 * count))
    owned = jnp.zeros((256, 1), F32)
    for i in range(n // 128):
        part = ids[:, i * 128 : (i + 1) * 128]
        begin = iota((256, 128), 0) * count
        hit = ((part >= begin) & (part < begin + count)).astype(F32)
        owned = owned + hit
    owned = jnp.max(jnp.sum(owned, axis=1, keepdims=True), axis=0, keepdims=True)
    longest = jnp.max(lines[1:17] - lines[0:16], axis=0, keepdims=True)
    over = (owned > SLOTS) | (longest > WINDOW)
    over_ref[...] = jnp.broadcast_to(over.astype(jnp.int32), over_ref.shape)
    lines = clip(lines)
    pl.semaphore_wait(barrier, 30)

    def first_send(k, to, frm):
        send(rows, line.at[inner], s1.at[k], r1.at[inner], inner_peer(to)).start()

    def first_done(k, to, frm):
        send(rows, line.at[frm], s1.at[k], r1.at[frm], inner_peer(to)).wait()

    others(inner, first_send)
    others(inner, first_done)
    compact = jnp.dot(pick, line[...].reshape(16 * SLOTS, d), preferred_element_type=F32).astype(BF16)
    window[...] = compact
    windows[outer] = compact
    half = pl.ds(pl.multiple_of(core * (WINDOW // 2), WINDOW // 2), WINDOW // 2)
    rest = pl.ds(pl.multiple_of((1 - core) * (WINDOW // 2), WINDOW // 2), WINDOW // 2)

    def second(k, to, frm):
        send(window.at[half], windows.at[outer, half], s2.at[k], r2.at[outer], outer_peer(to)).start()

    others(outer, second)
    partner = {"dev_2": 1 - core}

    def forward(k, to, frm):
        send(window.at[half], windows.at[frm, half], s2.at[k], r2.at[frm], outer_peer(to)).wait_recv()
        send(windows.at[frm, half], windows.at[frm, half], s3.at[k], r3.at[frm], partner).start()

    others(outer, forward)

    def last(k, to, frm):
        send(window.at[half], windows.at[frm, half], s2.at[k], r2.at[frm], outer_peer(to)).wait_send()
        copy = send(windows.at[frm, rest], windows.at[frm, rest], s3.at[k], r3.at[frm], partner)
        copy.wait_send()
        copy.wait_recv()

    others(outer, last)
    slot = iota((1, WINDOW), 1)
    places = []
    for g in range(16):
        place = lines[g : g + 1] + slot
        places.append(jnp.where(place < lines[g + 1 : g + 2], place, -1))
    source = windows[...].reshape(16 * WINDOW, d)
    for i in range(n // 128):
        row = iota((128, WINDOW), 0) + i * 128
        hot = cat([(row == place).astype(BF16) for place in places], 1)
        marks_ref[i * 128 : (i + 1) * 128, :] = jnp.dot(hot, source, preferred_element_type=F32).astype(BF16)


def gather_turn(ids, turn, points):
    d = points.shape[1]
    n = ids.shape[1]
    return pl.pallas_call(
        gather_kernel,
        out_shape=[jax.ShapeDtypeStruct((n, d), BF16), jax.ShapeDtypeStruct((8, 128), jnp.int32)],
        in_specs=[VMEM, VMEM, VMEM],
        out_specs=[VMEM, VMEM],
        scratch_shapes=[
            pltpu.VMEM((SLOTS, d), BF16),
            pltpu.VMEM((16, SLOTS, d), BF16),
            pltpu.VMEM((WINDOW, d), BF16),
            pltpu.VMEM((16, WINDOW, d), BF16),
        ]
        + [DMA((16,))] * 6,
        name="gather",
        compiler_params=pltpu.CompilerParams(
            collective_id=0, has_side_effects=True, vmem_limit_bytes=16 << 20
        ),
    )(ids, turn, points)


def gather_marks(points, ids):
    n = ids.shape[0]
    ids = ids.reshape(1, n)
    place = jnp.arange(n, dtype=jnp.int32)[:, None]

    def turn(low, high):
        bounds = jnp.stack([low, high]).astype(jnp.int32)
        return gather_turn(ids, jnp.broadcast_to(bounds[:, None], (2, 128)), points)

    marks, over = turn(jnp.int32(0), jnp.int32(n))

    def again(state):
        low, marks = state
        fresh = turn(low, low + SLOTS)[0]
        return low + SLOTS, jnp.where((place >= low) & (place < low + SLOTS), fresh, marks)

    return lax.while_loop(lambda s: s[0] < n, again, (jnp.where(over[0, 0] > 0, 0, n), marks))[1]


def raw_kernel(
    rows_total, points_ref, marks_ref, norm_ref, hi_ref, lo_ref, raw_ref, out_ref, own, mid, line, cross, s1, r1, s2, r2
):
    inner, outer = position()
    barrier = greet(inner, outer)
    rows, d = points_ref.shape
    n = marks_ref.shape[0]
    own[...] = jnp.zeros_like(own)

    def block(i, carry):
        here = pl.ds(pl.multiple_of(i * ROWS_STEP, ROWS_STEP), ROWS_STEP)
        pts = points_ref[here, :]
        nc = jnp.sum(jnp.square(pts.astype(F32)), axis=1, keepdims=True)
        g = lax.dot_general(pts, marks_ref[...], (((1,), (1,)), ((), ())), preferred_element_type=F32)
        ch, cl = split(jnp.exp((2.0 * g - nc - norm_ref[:1, :]) * (1.0 / (2.0 * d))))
        for j in range(n // 256):
            cols = slice(j * 256, (j + 1) * 256)
            k = (j + 1) * 256
            mul = lambda a, b: lax.dot_general(
                a, b, (((1,), (1,)), ((), ())), preferred_element_type=F32
            )
            x = mul(ch[:, :k], hi_ref[cols, :k])
            x += mul(cl[:, :k], hi_ref[cols, :k])
            x += mul(ch[:, :k], lo_ref[cols, :k])
            raw_ref[here, cols] = x
            for h in range(2):
                y = x[:, h * 128 : (h + 1) * 128]
                r = 2 * j + h
                own[r : r + 1, :] += jnp.sum(y, axis=0, keepdims=True)
                own[8 + r : 9 + r, :] += jnp.sum(jnp.square(y), axis=0, keepdims=True)
        return carry

    lax.fori_loop(0, rows // ROWS_STEP, block, 0)
    line[inner] = own[...]
    pl.semaphore_wait(barrier, 30)

    def first(k, to, frm):
        send(own, line.at[inner], s1.at[k], r1.at[inner], inner_peer(to)).start()

    def first_done(k, to, frm):
        send(own, line.at[frm], s1.at[k], r1.at[frm], inner_peer(to)).wait()

    others(inner, first)
    others(inner, first_done)
    total = jnp.sum(line[...], axis=0)
    mid[...] = total
    cross[outer] = total

    def second(k, to, frm):
        send(mid, cross.at[outer], s2.at[k], r2.at[outer], outer_peer(to)).start()

    def second_done(k, to, frm):
        send(mid, cross.at[frm], s2.at[k], r2.at[frm], outer_peer(to)).wait()

    others(outer, second)
    others(outer, second_done)
    total = jnp.sum(cross[...], axis=0) / rows_total
    mean = total[:8]
    out_ref[:8] = mean
    out_ref[8:] = lax.rsqrt(jnp.maximum(total[8:] - jnp.square(mean), 0.0) + 1e-05)


def raw_features(points, marks, norms, hi, lo, rows_total):
    rows = points.shape[0]
    n = marks.shape[0]
    shape = (16, n // 8)
    return pl.pallas_call(
        functools.partial(raw_kernel, rows_total),
        out_shape=[jax.ShapeDtypeStruct((rows, n), F32), jax.ShapeDtypeStruct(shape, F32)],
        in_specs=[VMEM] * 5,
        out_specs=[VMEM, VMEM],
        scratch_shapes=[
            pltpu.VMEM(shape, F32),
            pltpu.VMEM(shape, F32),
            pltpu.VMEM((16,) + shape, F32),
            pltpu.VMEM((16,) + shape, F32),
        ]
        + [DMA((16,))] * 4,
        name="raw",
        compiler_params=pltpu.CompilerParams(
            collective_id=1, has_side_effects=True, vmem_limit_bytes=40 << 20
        ),
    )(points, marks, norms, hi, lo)


def standardize_kernel(raw_ref, stats_ref, out_ref, buf, sems):
    steps = raw_ref.shape[0] // ROWS_STEP
    copies = []
    for s in range(steps):
        rows = slice(s * ROWS_STEP, (s + 1) * ROWS_STEP)
        if s >= 2:
            copies[s - 2].wait()
        for i in range(8):
            cols = slice(i * 128, (i + 1) * 128)
            x = raw_ref[rows, cols] - stats_ref[i : i + 1, :]
            buf[s % 2, :, cols] = (x * stats_ref[8 + i : 9 + i, :]).astype(BF16)
        copies.append(pltpu.make_async_copy(buf.at[s % 2], out_ref.at[rows, :], sems.at[s % 2]))
        copies[s].start()
    copies[steps - 2].wait()
    copies[steps - 1].wait()


def standardize(raw, stats):
    rows, n = raw.shape
    return pl.pallas_call(
        standardize_kernel,
        out_shape=jax.ShapeDtypeStruct((rows, n), BF16),
        in_specs=[VMEM, VMEM],
        out_specs=pl.BlockSpec(memory_space=pl.ANY),
        scratch_shapes=[pltpu.VMEM((2, ROWS_STEP, n), BF16), DMA((2,))],
        name="standardize",
        compiler_params=pltpu.CompilerParams(vmem_limit_bytes=16 << 20),
    )(raw, stats)


def shards(points, ridge, landmark_ids):
    marks = gather_marks(points, landmark_ids)
    hi, lo, norms = factor(marks, ridge)
    raw, stats = raw_features(points, marks, norms, hi, lo, points.shape[0] * lax.axis_size(GRP_DEV))
    return standardize(raw, stats)


def solution(mesh):
    torus = Mesh(
        mesh.devices.reshape(mesh.shape["grp"], 4, 8, 2), ("grp", "dev_0", "dev_1", "dev_2")
    )
    placed = (P(GRP_DEV, None), P(), P())
    return jax.shard_map(
        shards, mesh=torus, in_specs=placed, out_specs=P(GRP_DEV, None), check_vma=False
    )
```

time: 144 us -> 98.5 us (0.68)
  Pallas kernels: 127 us -> 96.2 us
  local copies, waits for them, and re-layouts: 8.83 us -> 1.07 us
  other arithmetic: 4.53 us -> 0.01 us
  between operations: 3.27 us -> 0.86 us
    pallas_call x1, Pallas kernels: 54.8 us -> 36.1 us  [factor(): pl.pallas_call(factor_kernel, out_shape=[jax.ShapeDtypeStruct((n, n), BF1...]
    pallas_call x5 -> x3, Pallas kernels: 72 us -> 60.1 us  [the longest x1 29.6 us: gather_turn(): pl.pallas_call(gather_kernel, out_shape=[jax.ShapeDtypeStruct((n, d), BF1...]
    unnamed x8 -> x2, local copies, waits for them, and re-layouts: 4.48 us -> 0.49 us
    reshape x1 -> x0, other arithmetic: 2.03 us -> none  [turn(): sel.reshape(SLOTS, 1)]
where the time goes in v3:
time: 98.5 us; the launch traced here: 98.3 us
  Pallas kernels  96.2 us (98%)
  local copies, waits for them, and re-layouts  1.07 us (1%)
    pallas_call x1, Pallas kernels, factor(): pl.pallas_call(factor_kernel, out_shape=[jax.ShapeDtypeStruct((n, n), BF1...  36.1 us
    pallas_call x1, Pallas kernels, gather_turn(): pl.pallas_call(gather_kernel, out_shape=[jax.ShapeDtypeStruct((n, d), BF1...  29.6 us
    pallas_call x1, Pallas kernels, raw_features(): pl.pallas_call(functools.partial(raw_kernel, rows_total), out_shape=[jax....  26.5 us
    pallas_call x1, Pallas kernels, standardize(): pl.pallas_call(standardize_kernel, out_shape=jax.ShapeDtypeStruct((rows,...  3.99 us

profile of v3, /device:TPU:1, one launch (start us, length us, event | category | flops | bytes accessed | tf_op | source)
XLA Modules:
  0.0 98.3 jit_solution(14821217938246503959)
XLA Ops:
  0.0 0.1 broadcast_in_dim.29.turn_ref
  0.1 29.6 %gather.2 = (bf16[1024,256]{1,0:T(8,128)(2,1)S(1)}, s32[8,128]{1,0:T(8,128)S(1)}) custom-call(s32[1,1024]{1,0:T(1,128)} %bitcast.10, s32[2,128]{1,0:T(2,128)S(1)} %broadcast_in_dim.29.turn_ref, bf16[2048,256]{1,0:T(8,128)(2,1)} %points_ref.3), custom_call_target="tpu_custom_call" | custom-call | tf_op jit(solution)/shard_map/gather/pallas_call | solution.py:318
  29.7 0.5 slice.3
  30.8 0.0 copy-start
  30.9 0.2 while.12
  31.1 0.5 copy-done
  31.5 36.1 %factor.1 = (bf16[1024,1024]{1,0:T(8,128)(2,1)S(1)}, bf16[1024,1024]{1,0:T(8,128)(2,1)S(1)}, f32[8,1024]{1,0:T(8,128)S(1)}) custom-call(bf16[1024,256]{1,0:T(8,128)(2,1)S(1)} %get-tuple-element.45.marks_ref, f32[1,1024]{1,0:T(1,128)S(1)} %bitcast.9), custom_call_target="tpu_custom_call" | custom-call | tf_op jit(solution)/shard_map/factor/pallas_call | solution.py:152
  67.6 26.5 %raw.1 = (f32[2048,1024]{1,0:T(8,128)S(1)}, f32[16,128]{1,0:T(8,128)S(1)}) custom-call(bf16[2048,256]{1,0:T(8,128)(2,1)} %get-tuple-element.127, bf16[1024,256]{1,0:T(8,128)(2,1)S(1)} %get-tuple-element.45.marks_ref, f32[8,1024]{1,0:T(8,128)S(1)} %get-tuple-element.46.norm_ref, bf16[1024,1024]{1,0:T(8,128)(2,1)S(1)} %get-tuple-element.47.hi_ref, ...), custom_call_target="tpu_custom_call" | custom-call | tf_op jit(solution)/shard_map/raw/pallas_call | solution.py:422
  94.1 4.0 %standardize.1 = bf16[2048,1024]{1,0:T(8,128)(2,1)} custom-call(f32[2048,1024]{1,0:T(8,128)S(1)} %get-tuple-element.49.raw_ref, f32[16,128]{1,0:T(8,128)S(1)} %get-tuple-element.50.stats_ref), custom_call_target="tpu_custom_call" | custom-call | tf_op jit(solution)/shard_map/standardize/pallas_call | solution.py:460
  (1 shorter events, 0.0 us)
Async XLA Ops:
  30.8 0.7 copy-start

commit v4 on v3

--- a/solution.py
+++ b/solution.py
@@ -90,40 +90,42 @@
     return cat([v] + v2, 0)
 
 
-def factor_kernel(marks_ref, ridge_ref, hi_ref, lo_ref, norm_ref, m, rt, rh, rl):
+def factor_kernel(marks_ref, ridge_ref, hi_ref, lo_ref, norm_ref, m, diag, inv, rt, rh, rl):
     n, d = marks_ref.shape
     nb = n // BLK
     eye = (
         lax.broadcasted_iota(jnp.int32, (BLK, BLK), 0)
         == lax.broadcasted_iota(jnp.int32, (BLK, BLK), 1)
     ).astype(F32)
+    column = lax.broadcasted_iota(jnp.int32, (BLK, n), 1)
     sq = jnp.square(marks_ref[...].astype(F32))
     nr = lax.dot_general(
         jnp.ones((8, d), F32), sq, (((1,), (1,)), ((), ())), preferred_element_type=F32, precision=HI
     )
     norm_ref[...] = nr
-    for i in range(nb):
+
+    def core_rows(i):
         rows = slice(i * BLK, (i + 1) * BLK)
         blk = marks_ref[rows, :]
         nc = jnp.sum(jnp.square(blk.astype(F32)), axis=1, keepdims=True)
         g = lax.dot_general(blk, marks_ref[...], (((1,), (1,)), ((), ())), preferred_element_type=F32)
         m[rows, :] = jnp.exp((2.0 * g - nc - nr[:1]) * (1.0 / (2.0 * d)))
         m[rows, rows] += eye * ridge_ref[:, rows]
-    rt[...] = jnp.zeros_like(rt)
-    rh[...] = jnp.zeros_like(rh)
-    rl[...] = jnp.zeros_like(rl)
-
-    def step(j, carry):
+
+    def finish_row(j):
         here = pl.ds(pl.multiple_of(j * BLK, BLK), BLK)
-        linv = inverse_factor(m[here, here], eye)
-        for i in range(1, nb):
-            rows = slice(i * BLK, (i + 1) * BLK)
-            m[rows, :] = m[rows, :] - pair_dot(rt[rows, :], rh[...], rl[...])
         m[here, here] = eye
         high, low = split(m[here, :])
-        r = pair_dot(cat(split(linv), 1), cat([high, high], 0), cat([low, low], 0))
-        m[here, :] = r
+        r = pair_dot(cat(split(inv[...]), 1), cat([high, high], 0), cat([low, low], 0))
         high, low = split(r)
+        keep = column < (j + 1) * BLK
+        hi_ref[here, :] = jnp.where(keep, high, jnp.zeros_like(high))
+        lo_ref[here, :] = jnp.where(keep, low, jnp.zeros_like(low))
+        return r, high, low
+
+    def update_rows(j):
+        here = pl.ds(pl.multiple_of(j * BLK, BLK), BLK)
+        r, high, low = finish_row(j)
         rh[:BLK, :] = high
         rh[BLK:, :] = high
         rl[:BLK, :] = low
@@ -131,20 +133,39 @@
         for i in range(1, nb):
             rows = slice(i * BLK, (i + 1) * BLK)
             m[rows, here] = jnp.where(i > j, 0.0, m[rows, here])
-            high, low = split(jnp.where(i > j + 1, r[:, rows].T, 0.0))
+            high, low = split(jnp.where(i > j, r[:, rows].T, 0.0))
             rt[rows, :BLK] = high
             rt[rows, BLK:] = low
+        for i in range(1, nb):
+            rows = slice(i * BLK, (i + 1) * BLK)
+            m[rows, :] = m[rows, :] - pair_dot(rt[rows, :], rh[...], rl[...])
+
+    def next_diagonal(j, linv):
+        here = pl.ds(pl.multiple_of(j * BLK, BLK), BLK)
         after = pl.ds(pl.multiple_of(jnp.minimum(j + 1, nb - 1) * BLK, BLK), BLK)
-        t = jnp.where(j + 1 < nb, m[here, after].T, 0.0)
-        m[after, :] = m[after, :] - pair_dot(cat(split(t), 1), rh[...], rl[...])
+        high, low = split(m[here, after])
+        u = pair_dot(cat(split(linv), 1), cat([high, high], 0), cat([low, low], 0))
+        high, low = split(u)
+        t = u.T
+        diag[...] = m[after, after] - pair_dot(
+            cat(split(t), 1), cat([high, high], 0), cat([low, low], 0)
+        )
+        inv[...] = linv
+
+    core_rows(0)
+    linv = inverse_factor(m[:BLK, :BLK], eye)
+    for i in range(1, nb):
+        core_rows(i)
+    next_diagonal(0, linv)
+
+    def step(j, carry):
+        linv = inverse_factor(diag[...], eye)
+        update_rows(j - 1)
+        next_diagonal(j, linv)
         return carry
 
-    lax.fori_loop(0, nb, step, 0)
-    for i in range(nb):
-        rows = slice(i * BLK, (i + 1) * BLK)
-        x = m[rows, :]
-        x = jnp.where(lax.broadcasted_iota(jnp.int32, x.shape, 1) < (i + 1) * BLK, x, 0.0)
-        hi_ref[rows, :], lo_ref[rows, :] = split(x)
+    lax.fori_loop(1, nb, step, 0)
+    finish_row(nb - 1)
 
 
 def factor(marks, ridge):
@@ -160,6 +181,8 @@
         out_specs=[VMEM, VMEM, VMEM],
         scratch_shapes=[
             pltpu.VMEM((n, n), F32),
+            pltpu.VMEM((BLK, BLK), F32),
+            pltpu.VMEM((BLK, BLK), F32),
             pltpu.VMEM((n, 2 * BLK), BF16),
             pltpu.VMEM((2 * BLK, n), BF16),
             pltpu.VMEM((2 * BLK, n), BF16),
@@ -222,7 +245,7 @@
 
 
 def gather_kernel(
-    ids_ref, turn_ref, points_ref, marks_ref, over_ref, rows, line, window, windows, s1, r1, s2, r2, s3, r3
+    ids_ref, turn_ref, points_ref, marks_ref, over_ref, rows, line, window, windows, hot, s1, r1, s2, r2, s3, r3
 ):
     inner, outer = position()
     core = lax.rem(inner, 2)
@@ -242,8 +265,9 @@
     sel = jnp.sum(jnp.where(wanted, ids - start + 1, 0).astype(F32), axis=1, keepdims=True) - 1.0
     pick = (iota((SLOTS, count), 1).astype(F32) == sel).astype(BF16)
     picked = jnp.dot(pick, points_ref[...], preferred_element_type=F32).astype(BF16)
-    rows[...] = picked
-    line[inner] = picked
+    rows[0] = picked[:, :128]
+    rows[1] = picked[:, 128:]
+    line[inner] = rows[core]
     at = clip(count_below(ids, (outer * 16 + iota((24, n), 0)) * count))
     slot = iota((1, 16 * SLOTS), 1)
     place, limit = slot, slot
@@ -268,48 +292,52 @@
     pl.semaphore_wait(barrier, 30)
 
     def first_send(k, to, frm):
-        send(rows, line.at[inner], s1.at[k], r1.at[inner], inner_peer(to)).start()
+        send(rows.at[lax.rem(to, 2)], line.at[inner], s1.at[k], r1.at[inner], inner_peer(to)).start()
 
     def first_done(k, to, frm):
-        send(rows, line.at[frm], s1.at[k], r1.at[frm], inner_peer(to)).wait()
+        send(rows.at[lax.rem(to, 2)], line.at[frm], s1.at[k], r1.at[frm], inner_peer(to)).wait()
 
     others(inner, first_send)
-    others(inner, first_done)
-    compact = jnp.dot(pick, line[...].reshape(16 * SLOTS, d), preferred_element_type=F32).astype(BF16)
-    window[...] = compact
-    windows[outer] = compact
-    half = pl.ds(pl.multiple_of(core * (WINDOW // 2), WINDOW // 2), WINDOW // 2)
-    rest = pl.ds(pl.multiple_of((1 - core) * (WINDOW // 2), WINDOW // 2), WINDOW // 2)
-
-    def second(k, to, frm):
-        send(window.at[half], windows.at[outer, half], s2.at[k], r2.at[outer], outer_peer(to)).start()
-
-    others(outer, second)
-    partner = {"dev_2": 1 - core}
-
-    def forward(k, to, frm):
-        send(window.at[half], windows.at[frm, half], s2.at[k], r2.at[frm], outer_peer(to)).wait_recv()
-        send(windows.at[frm, half], windows.at[frm, half], s3.at[k], r3.at[frm], partner).start()
-
-    others(outer, forward)
-
-    def last(k, to, frm):
-        send(window.at[half], windows.at[frm, half], s2.at[k], r2.at[frm], outer_peer(to)).wait_send()
-        copy = send(windows.at[frm, rest], windows.at[frm, rest], s3.at[k], r3.at[frm], partner)
-        copy.wait_send()
-        copy.wait_recv()
-
-    others(outer, last)
     slot = iota((1, WINDOW), 1)
     places = []
     for g in range(16):
         place = lines[g : g + 1] + slot
         places.append(jnp.where(place < lines[g + 1 : g + 2], place, -1))
-    source = windows[...].reshape(16 * WINDOW, d)
     for i in range(n // 128):
         row = iota((128, WINDOW), 0) + i * 128
-        hot = cat([(row == place).astype(BF16) for place in places], 1)
-        marks_ref[i * 128 : (i + 1) * 128, :] = jnp.dot(hot, source, preferred_element_type=F32).astype(BF16)
+        hot[i * 128 : (i + 1) * 128, :] = cat([(row == place).astype(BF16) for place in places], 1)
+    others(inner, first_done)
+    compact = jnp.dot(pick, line[...].reshape(16 * SLOTS, 128), preferred_element_type=F32).astype(BF16)
+    window[...] = compact
+    windows[core, outer] = compact
+    partner = {"dev_2": 1 - core}
+
+    def second(k, to, frm):
+        send(window, windows.at[core, outer], s2.at[k], r2.at[outer], outer_peer(to)).start()
+
+    others(outer, second)
+    send(window, windows.at[core, outer], s3.at[0], r3.at[outer], partner).start()
+
+    def forward(k, to, frm):
+        send(window, windows.at[core, frm], s2.at[k], r2.at[frm], outer_peer(to)).wait_recv()
+        send(windows.at[core, frm], windows.at[core, frm], s3.at[k], r3.at[frm], partner).start()
+
+    others(outer, forward)
+
+    def last(k, to, frm):
+        send(window, windows.at[core, frm], s2.at[k], r2.at[frm], outer_peer(to)).wait_send()
+        copy = send(windows.at[1 - core, frm], windows.at[1 - core, frm], s3.at[k], r3.at[frm], partner)
+        copy.wait_send()
+        copy.wait_recv()
+
+    copy = send(window, windows.at[1 - core, outer], s3.at[0], r3.at[outer], partner)
+    copy.wait_send()
+    copy.wait_recv()
+    others(outer, last)
+    source = cat([windows[0].reshape(16 * WINDOW, 128), windows[1].reshape(16 * WINDOW, 128)], 1)
+    for i in range(n // 256):
+        part = slice(i * 256, (i + 1) * 256)
+        marks_ref[part, :] = jnp.dot(hot[part, :], source, preferred_element_type=F32).astype(BF16)
 
 
 def gather_turn(ids, turn, points):
@@ -321,15 +349,16 @@
         in_specs=[VMEM, VMEM, VMEM],
         out_specs=[VMEM, VMEM],
         scratch_shapes=[
-            pltpu.VMEM((SLOTS, d), BF16),
-            pltpu.VMEM((16, SLOTS, d), BF16),
-            pltpu.VMEM((WINDOW, d), BF16),
-            pltpu.VMEM((16, WINDOW, d), BF16),
+            pltpu.VMEM((2, SLOTS, d // 2), BF16),
+            pltpu.VMEM((16, SLOTS, d // 2), BF16),
+            pltpu.VMEM((WINDOW, d // 2), BF16),
+            pltpu.VMEM((2, 16, WINDOW, d // 2), BF16),
+            pltpu.VMEM((n, 16 * WINDOW), BF16),
         ]
         + [DMA((16,))] * 6,
         name="gather",
         compiler_params=pltpu.CompilerParams(
-            collective_id=0, has_side_effects=True, vmem_limit_bytes=16 << 20
+            collective_id=0, has_side_effects=True, vmem_limit_bytes=24 << 20
         ),
     )(ids, turn, points)
 
@@ -357,7 +386,14 @@
     rows_total, points_ref, marks_ref, norm_ref, hi_ref, lo_ref, raw_ref, out_ref, own, mid, line, cross, s1, r1, s2, r2
 ):
     inner, outer = position()
+    core = lax.rem(inner, 2)
     barrier = greet(inner, outer)
+    cross_peer = lambda o, c: {"grp": lax.div(o, 4), "dev_0": lax.rem(o, 4), "dev_2": c}
+
+    def greet_cross(k, to, frm):
+        pl.semaphore_signal(barrier, inc=1, device_id=cross_peer(to, 1 - core), device_id_type=MESH_IDS)
+
+    others(outer, greet_cross)
     rows, d = points_ref.shape
     n = marks_ref.shape[0]
     own[...] = jnp.zeros_like(own)
@@ -381,38 +417,43 @@
             for h in range(2):
                 y = x[:, h * 128 : (h + 1) * 128]
                 r = 2 * j + h
-                own[r : r + 1, :] += jnp.sum(y, axis=0, keepdims=True)
-                own[8 + r : 9 + r, :] += jnp.sum(jnp.square(y), axis=0, keepdims=True)
+                own[0, r : r + 1, :] += jnp.sum(y, axis=0, keepdims=True)
+                own[1, r : r + 1, :] += jnp.sum(jnp.square(y), axis=0, keepdims=True)
         return carry
 
     lax.fori_loop(0, rows // ROWS_STEP, block, 0)
-    line[inner] = own[...]
-    pl.semaphore_wait(barrier, 30)
+    line[inner] = own[core]
+    pl.semaphore_wait(barrier, 45)
 
     def first(k, to, frm):
-        send(own, line.at[inner], s1.at[k], r1.at[inner], inner_peer(to)).start()
+        send(own.at[lax.rem(to, 2)], line.at[inner], s1.at[k], r1.at[inner], inner_peer(to)).start()
 
     def first_done(k, to, frm):
-        send(own, line.at[frm], s1.at[k], r1.at[frm], inner_peer(to)).wait()
+        send(own.at[lax.rem(to, 2)], line.at[frm], s1.at[k], r1.at[frm], inner_peer(to)).wait()
 
     others(inner, first)
     others(inner, first_done)
     total = jnp.sum(line[...], axis=0)
     mid[...] = total
-    cross[outer] = total
+    cross[core, outer] = total
+    partner = {"dev_2": 1 - core}
 
     def second(k, to, frm):
-        send(mid, cross.at[outer], s2.at[k], r2.at[outer], outer_peer(to)).start()
+        for c in (core, 1 - core):
+            send(mid, cross.at[core, outer], s2.at[c, k], r2.at[core, outer], cross_peer(to, c)).start()
 
     def second_done(k, to, frm):
-        send(mid, cross.at[frm], s2.at[k], r2.at[frm], outer_peer(to)).wait()
+        for c in (core, 1 - core):
+            send(mid, cross.at[c, frm], s2.at[c, k], r2.at[c, frm], cross_peer(to, c)).wait()
 
     others(outer, second)
+    send(mid, cross.at[core, outer], s2.at[1 - core, 0], r2.at[core, outer], partner).start()
+    send(mid, cross.at[1 - core, outer], s2.at[1 - core, 0], r2.at[1 - core, outer], partner).wait()
     others(outer, second_done)
-    total = jnp.sum(cross[...], axis=0) / rows_total
-    mean = total[:8]
+    mean = jnp.sum(cross[0], axis=0) / rows_total
+    squares = jnp.sum(cross[1], axis=0) / rows_total
     out_ref[:8] = mean
-    out_ref[8:] = lax.rsqrt(jnp.maximum(total[8:] - jnp.square(mean), 0.0) + 1e-05)
+    out_ref[8:] = lax.rsqrt(jnp.maximum(squares - jnp.square(mean), 0.0) + 1e-05)
 
 
 def raw_features(points, marks, norms, hi, lo, rows_total):
@@ -425,12 +466,13 @@
         in_specs=[VMEM] * 5,
         out_specs=[VMEM, VMEM],
         scratch_shapes=[
-            pltpu.VMEM(shape, F32),
-            pltpu.VMEM(shape, F32),
-            pltpu.VMEM((16,) + shape, F32),
-            pltpu.VMEM((16,) + shape, F32),
+            pltpu.VMEM((2, 8, n // 8), F32),
+            pltpu.VMEM((8, n // 8), F32),
+            pltpu.VMEM((16, 8, n // 8), F32),
+            pltpu.VMEM((2, 16, 8, n // 8), F32),
         ]
-        + [DMA((16,))] * 4,
+        + [DMA((16,))] * 2
+        + [DMA((2, 16))] * 2,
         name="raw",
         compiler_params=pltpu.CompilerParams(
             collective_id=1, has_side_effects=True, vmem_limit_bytes=40 << 20

time: 98.5 us -> 94.8 us (0.962)
  Pallas kernels: 96.2 us -> 92.5 us
    pallas_call x1, Pallas kernels: 36.1 us -> 32.9 us  [factor(): pl.pallas_call(factor_kernel, out_shape=[jax.ShapeDtypeStruct((n, n), BF1...]
where the time goes in v4:
time: 94.8 us; the launch traced here: 94.6 us
  Pallas kernels  92.5 us (98%)
  local copies, waits for them, and re-layouts  1.07 us (1%)
    pallas_call x1, Pallas kernels, factor(): pl.pallas_call(factor_kernel, out_shape=[jax.ShapeDtypeStruct((n, n), BF1...  32.9 us
    pallas_call x1, Pallas kernels, gather_turn(): pl.pallas_call(gather_kernel, out_shape=[jax.ShapeDtypeStruct((n, d), BF1...  28.8 us
    pallas_call x1, Pallas kernels, raw_features(): pl.pallas_call(functools.partial(raw_kernel, rows_total), out_shape=[jax....  26.9 us
    pallas_call x1, Pallas kernels, standardize(): pl.pallas_call(standardize_kernel, out_shape=jax.ShapeDtypeStruct((rows,...  3.99 us

profile of v4, /device:TPU:1, one launch (start us, length us, event | category | flops | bytes accessed | tf_op | source)
XLA Modules:
  0.0 94.6 jit_solution(14427368021669684579)
XLA Ops:
  0.0 0.1 broadcast_in_dim.29.turn_ref
  0.1 28.8 %gather.2 = (bf16[1024,256]{1,0:T(8,128)(2,1)S(1)}, s32[8,128]{1,0:T(8,128)S(1)}) custom-call(s32[1,1024]{1,0:T(1,128)} %bitcast.10, s32[2,128]{1,0:T(2,128)S(1)} %broadcast_in_dim.29.turn_ref, bf16[2048,256]{1,0:T(8,128)(2,1)} %points_ref.3), custom_call_target="tpu_custom_call" | custom-call | tf_op jit(solution)/shard_map/gather/pallas_call | solution.py:346
  28.8 0.5 slice.3
  30.0 0.0 copy-start
  30.0 0.2 while.12
  30.2 0.5 copy-done
  30.7 32.9 %factor.1 = (bf16[1024,1024]{1,0:T(8,128)(2,1)S(1)}, bf16[1024,1024]{1,0:T(8,128)(2,1)S(1)}, f32[8,1024]{1,0:T(8,128)S(1)}) custom-call(bf16[1024,256]{1,0:T(8,128)(2,1)S(1)} %get-tuple-element.45.marks_ref, f32[1,1024]{1,0:T(1,128)S(1)} %bitcast.9), custom_call_target="tpu_custom_call" | custom-call | tf_op jit(solution)/shard_map/factor/pallas_call | solution.py:173
  63.6 26.9 %raw.1 = (f32[2048,1024]{1,0:T(8,128)S(1)}, f32[16,128]{1,0:T(8,128)S(1)}) custom-call(bf16[2048,256]{1,0:T(8,128)(2,1)} %get-tuple-element.127, bf16[1024,256]{1,0:T(8,128)(2,1)S(1)} %get-tuple-element.45.marks_ref, f32[8,1024]{1,0:T(8,128)S(1)} %get-tuple-element.46.norm_ref, bf16[1024,1024]{1,0:T(8,128)(2,1)S(1)} %get-tuple-element.47.hi_ref, ...), custom_call_target="tpu_custom_call" | custom-call | tf_op jit(solution)/shard_map/raw/pallas_call | solution.py:463
  90.5 4.0 %standardize.1 = bf16[2048,1024]{1,0:T(8,128)(2,1)} custom-call(f32[2048,1024]{1,0:T(8,128)S(1)} %get-tuple-element.49.raw_ref, f32[16,128]{1,0:T(8,128)S(1)} %get-tuple-element.50.stats_ref), custom_call_target="tpu_custom_call" | custom-call | tf_op jit(solution)/shard_map/standardize/pallas_call | solution.py:502
  (1 shorter events, 0.0 us)
Async XLA Ops:
  30.0 0.7 copy-start

commit v5 on v4

--- a/solution.py
+++ b/solution.py
@@ -13,7 +13,8 @@
 BF16 = jnp.bfloat16
 HI = lax.Precision.HIGHEST
 BLK = 128
-ROWS_STEP = 256
+ROWS_STEP = 1024
+OUT_STEP = 256
 VMEM = pl.BlockSpec(memory_space=pltpu.VMEM)
 
 
@@ -213,11 +214,8 @@
 
 
 def others(me, body):
-    def step(k, carry):
+    for k in range(1, 16):
         body(k, lax.rem(me + k, 16), lax.rem(me + 16 - k, 16))
-        return carry
-
-    lax.fori_loop(1, 16, step, 0)
 
 
 def greet(inner, outer):
@@ -481,10 +479,10 @@
 
 
 def standardize_kernel(raw_ref, stats_ref, out_ref, buf, sems):
-    steps = raw_ref.shape[0] // ROWS_STEP
+    steps = raw_ref.shape[0] // OUT_STEP
     copies = []
     for s in range(steps):
-        rows = slice(s * ROWS_STEP, (s + 1) * ROWS_STEP)
+        rows = slice(s * OUT_STEP, (s + 1) * OUT_STEP)
         if s >= 2:
             copies[s - 2].wait()
         for i in range(8):
@@ -504,7 +502,7 @@
         out_shape=jax.ShapeDtypeStruct((rows, n), BF16),
         in_specs=[VMEM, VMEM],
         out_specs=pl.BlockSpec(memory_space=pl.ANY),
-        scratch_shapes=[pltpu.VMEM((2, ROWS_STEP, n), BF16), DMA((2,))],
+        scratch_shapes=[pltpu.VMEM((2, OUT_STEP, n), BF16), DMA((2,))],
         name="standardize",
         compiler_params=pltpu.CompilerParams(vmem_limit_bytes=16 << 20),
     )(raw, stats)

time: 94.8 us -> 92.3 us (0.974)
  Pallas kernels: 92.5 us -> 90 us
    pallas_call x1, Pallas kernels: 26.9 us -> 24.2 us  [raw_features(): pl.pallas_call(functools.partial(raw_kernel, rows_total), out_shape=[jax....]
where the time goes in v5:
time: 92.3 us; the launch traced here: 92.1 us
  Pallas kernels  90 us (98%)
  local copies, waits for them, and re-layouts  1.25 us (1%)
    pallas_call x1, Pallas kernels, factor(): pl.pallas_call(factor_kernel, out_shape=[jax.ShapeDtypeStruct((n, n), BF1...  33.1 us
    pallas_call x1, Pallas kernels, gather_turn(): pl.pallas_call(gather_kernel, out_shape=[jax.ShapeDtypeStruct((n, d), BF1...  28.7 us
    pallas_call x1, Pallas kernels, raw_features(): pl.pallas_call(functools.partial(raw_kernel, rows_total), out_shape=[jax....  24.2 us
    pallas_call x1, Pallas kernels, standardize(): pl.pallas_call(standardize_kernel, out_shape=jax.ShapeDtypeStruct((rows,...  3.99 us

profile of v5, /device:TPU:1, one launch (start us, length us, event | category | flops | bytes accessed | tf_op | source)
XLA Modules:
  0.0 92.1 jit_solution(5164668544670114562)
XLA Ops:
  0.0 0.1 broadcast_in_dim.29.turn_ref
  0.1 28.7 %gather.2 = (bf16[1024,256]{1,0:T(8,128)(2,1)S(1)}, s32[8,128]{1,0:T(8,128)S(1)}) custom-call(s32[1,1024]{1,0:T(1,128)} %bitcast.10, s32[2,128]{1,0:T(2,128)S(1)} %broadcast_in_dim.29.turn_ref, bf16[2048,256]{1,0:T(8,128)(2,1)} %points_ref.3), custom_call_target="tpu_custom_call" | custom-call | tf_op jit(solution)/shard_map/gather/pallas_call | solution.py:344
  28.8 0.5 slice.3
  30.0 0.0 copy-start
  30.0 0.7 copy-done
  30.7 33.1 %factor.1 = (bf16[1024,1024]{1,0:T(8,128)(2,1)S(1)}, bf16[1024,1024]{1,0:T(8,128)(2,1)S(1)}, f32[8,1024]{1,0:T(8,128)S(1)}) custom-call(bf16[1024,256]{1,0:T(8,128)(2,1)S(1)} %get-tuple-element.45.marks_ref, f32[1,1024]{1,0:T(1,128)S(1)} %bitcast.9), custom_call_target="tpu_custom_call" | custom-call | tf_op jit(solution)/shard_map/factor/pallas_call | solution.py:174
  63.7 24.2 %raw.1 = (f32[2048,1024]{1,0:T(8,128)S(1)}, f32[16,128]{1,0:T(8,128)S(1)}) custom-call(bf16[2048,256]{1,0:T(8,128)(2,1)} %get-tuple-element.127, bf16[1024,256]{1,0:T(8,128)(2,1)S(1)} %get-tuple-element.45.marks_ref, f32[8,1024]{1,0:T(8,128)S(1)} %get-tuple-element.46.norm_ref, bf16[1024,1024]{1,0:T(8,128)(2,1)S(1)} %get-tuple-element.47.hi_ref, ...), custom_call_target="tpu_custom_call" | custom-call | tf_op jit(solution)/shard_map/raw/pallas_call | solution.py:461
  88.0 4.0 %standardize.1 = bf16[2048,1024]{1,0:T(8,128)(2,1)} custom-call(f32[2048,1024]{1,0:T(8,128)S(1)} %get-tuple-element.49.raw_ref, f32[16,128]{1,0:T(8,128)S(1)} %get-tuple-element.50.stats_ref), custom_call_target="tpu_custom_call" | custom-call | tf_op jit(solution)/shard_map/standardize/pallas_call | solution.py:500
  (2 shorter events, 0.0 us)
Async XLA Ops:
  30.0 0.7 copy-start

commit v6 on v5

--- a/solution.py
+++ b/solution.py
@@ -31,6 +31,7 @@
     for q in range(8):
         b = [[lane(g1[t], lane0 + 8 * q + c) for t in range(q, 8)] for c in range(8)]
         root = None
+        held = []
         scale, inverse, last_scale, last_inverse = None, None, None, None
         for k in range(8):
             p = sub(b[k][0], k)
@@ -54,9 +55,15 @@
                     inverse, last_inverse = next_inverse, inverse
             a1 = sub(g1[q], k)
             a2 = sub(g2[q], k)
-            for t in range(q, 8):
-                g1[t] = g1[t] - m[t - q] * a1
-                g2[t] = g2[t] - m[t - q] * a2
+            g1[q] = g1[q] - m[0] * a1
+            g2[q] = g2[q] - m[0] * a2
+            held.append((m, a1, a2))
+        for t in range(q + 1, 8):
+            for g, w in ((g1, 1), (g2, 2)):
+                terms = [h[0][t - q] * h[w] for h in held]
+                while len(terms) > 1:
+                    terms = [x + y for x, y in zip(terms[::2], terms[1::2])]
+                g[t] = g[t] - terms[0]
         g1[q] = g1[q] * root
         g2[q] = g2[q] * root
     return g1, g2
@@ -196,6 +203,7 @@
 MESH_IDS = pl.DeviceIdType.MESH
 SLOTS = 16
 WINDOW = 128
+SENT = 96
 DMA = pltpu.SemaphoreType.DMA
 
 
@@ -243,10 +251,12 @@
 
 
 def gather_kernel(
-    ids_ref, turn_ref, points_ref, marks_ref, over_ref, rows, line, window, windows, hot, s1, r1, s2, r2, s3, r3
+    ids_ref, turn_ref, points_ref, marks_ref, over_ref, pts, rows, line, window, windows, hot, s0, s1, r1, s2, r2, s3, r3
 ):
     inner, outer = position()
     core = lax.rem(inner, 2)
+    fetch = pltpu.make_async_copy(points_ref, pts, s0)
+    fetch.start()
     barrier = greet(inner, outer)
     count, d = points_ref.shape
     n = marks_ref.shape[0]
@@ -254,6 +264,7 @@
     ids = ids_ref[...]
     low, high = turn_ref[0:1, 0:1], turn_ref[1:2, 0:1]
     clip = lambda x: jnp.minimum(jnp.maximum(x, low), high)
+    windows[:, :, SENT:, :] = jnp.zeros((2, 16, WINDOW - SENT, 128), BF16)
     start = (outer * 16 + inner) * count
     first = clip(count_below(ids, jnp.full((1, n), start)))
     mark = iota((SLOTS, n), 1)
@@ -262,7 +273,8 @@
     )
     sel = jnp.sum(jnp.where(wanted, ids - start + 1, 0).astype(F32), axis=1, keepdims=True) - 1.0
     pick = (iota((SLOTS, count), 1).astype(F32) == sel).astype(BF16)
-    picked = jnp.dot(pick, points_ref[...], preferred_element_type=F32).astype(BF16)
+    fetch.wait()
+    picked = jnp.dot(pick, pts[...], preferred_element_type=F32).astype(BF16)
     rows[0] = picked[:, :128]
     rows[1] = picked[:, 128:]
     line[inner] = rows[core]
@@ -284,7 +296,7 @@
         owned = owned + hit
     owned = jnp.max(jnp.sum(owned, axis=1, keepdims=True), axis=0, keepdims=True)
     longest = jnp.max(lines[1:17] - lines[0:16], axis=0, keepdims=True)
-    over = (owned > SLOTS) | (longest > WINDOW)
+    over = (owned > SLOTS) | (longest > SENT)
     over_ref[...] = jnp.broadcast_to(over.astype(jnp.int32), over_ref.shape)
     lines = clip(lines)
     pl.semaphore_wait(barrier, 30)
@@ -307,28 +319,29 @@
     others(inner, first_done)
     compact = jnp.dot(pick, line[...].reshape(16 * SLOTS, 128), preferred_element_type=F32).astype(BF16)
     window[...] = compact
-    windows[core, outer] = compact
+    windows[core, outer, :SENT] = compact[:SENT]
+    kept = pl.ds(0, SENT)
     partner = {"dev_2": 1 - core}
 
     def second(k, to, frm):
-        send(window, windows.at[core, outer], s2.at[k], r2.at[outer], outer_peer(to)).start()
+        send(window.at[kept], windows.at[core, outer, kept], s2.at[k], r2.at[outer], outer_peer(to)).start()
 
     others(outer, second)
-    send(window, windows.at[core, outer], s3.at[0], r3.at[outer], partner).start()
+    send(window.at[kept], windows.at[core, outer, kept], s3.at[0], r3.at[outer], partner).start()
 
     def forward(k, to, frm):
-        send(window, windows.at[core, frm], s2.at[k], r2.at[frm], outer_peer(to)).wait_recv()
-        send(windows.at[core, frm], windows.at[core, frm], s3.at[k], r3.at[frm], partner).start()
+        send(window.at[kept], windows.at[core, frm, kept], s2.at[k], r2.at[frm], outer_peer(to)).wait_recv()
+        send(windows.at[core, frm, kept], windows.at[core, frm, kept], s3.at[k], r3.at[frm], partner).start()
 
     others(outer, forward)
 
     def last(k, to, frm):
-        send(window, windows.at[core, frm], s2.at[k], r2.at[frm], outer_peer(to)).wait_send()
-        copy = send(windows.at[1 - core, frm], windows.at[1 - core, frm], s3.at[k], r3.at[frm], partner)
+        send(window.at[kept], windows.at[core, frm, kept], s2.at[k], r2.at[frm], outer_peer(to)).wait_send()
+        copy = send(windows.at[1 - core, frm, kept], windows.at[1 - core, frm, kept], s3.at[k], r3.at[frm], partner)
         copy.wait_send()
         copy.wait_recv()
 
-    copy = send(window, windows.at[1 - core, outer], s3.at[0], r3.at[outer], partner)
+    copy = send(window.at[kept], windows.at[1 - core, outer, kept], s3.at[0], r3.at[outer], partner)
     copy.wait_send()
     copy.wait_recv()
     others(outer, last)
@@ -344,14 +357,16 @@
     return pl.pallas_call(
         gather_kernel,
         out_shape=[jax.ShapeDtypeStruct((n, d), BF16), jax.ShapeDtypeStruct((8, 128), jnp.int32)],
-        in_specs=[VMEM, VMEM, VMEM],
+        in_specs=[VMEM, VMEM, pl.BlockSpec(memory_space=pl.ANY)],
         out_specs=[VMEM, VMEM],
         scratch_shapes=[
+            pltpu.VMEM(points.shape, BF16),
             pltpu.VMEM((2, SLOTS, d // 2), BF16),
             pltpu.VMEM((16, SLOTS, d // 2), BF16),
             pltpu.VMEM((WINDOW, d // 2), BF16),
             pltpu.VMEM((2, 16, WINDOW, d // 2), BF16),
             pltpu.VMEM((n, 16 * WINDOW), BF16),
+            DMA,
         ]
         + [DMA((16,))] * 6,
         name="gather",

time: 92.3 us -> 89.7 us (0.972)
  Pallas kernels: 90 us -> 87.4 us
    pallas_call x1, Pallas kernels: 28.7 us -> 26.8 us  [gather_turn(): pl.pallas_call(gather_kernel, out_shape=[jax.ShapeDtypeStruct((n, d), BF1...]
where the time goes in v6:
time: 89.7 us; the launch traced here: 89.5 us
  Pallas kernels  87.4 us (97%)
  local copies, waits for them, and re-layouts  1.25 us (1%)
    pallas_call x1, Pallas kernels, factor(): pl.pallas_call(factor_kernel, out_shape=[jax.ShapeDtypeStruct((n, n), BF1...  32.8 us
    pallas_call x1, Pallas kernels, gather_turn(): pl.pallas_call(gather_kernel, out_shape=[jax.ShapeDtypeStruct((n, d), BF1...  26.8 us
    pallas_call x1, Pallas kernels, raw_features(): pl.pallas_call(functools.partial(raw_kernel, rows_total), out_shape=[jax....  23.8 us
    pallas_call x1, Pallas kernels, standardize(): pl.pallas_call(standardize_kernel, out_shape=jax.ShapeDtypeStruct((rows,...  3.99 us

profile of v6, /device:TPU:1, one launch (start us, length us, event | category | flops | bytes accessed | tf_op | source)
XLA Modules:
  0.0 89.5 jit_solution(375289741077150329)
XLA Ops:
  0.0 0.1 broadcast_in_dim.29.turn_ref
  0.1 26.8 %gather.2 = (bf16[1024,256]{1,0:T(8,128)(2,1)S(1)}, s32[8,128]{1,0:T(8,128)S(1)}) custom-call(s32[1,1024]{1,0:T(1,128)} %bitcast.10, s32[2,128]{1,0:T(2,128)S(1)} %broadcast_in_dim.29.turn_ref, bf16[2048,256]{1,0:T(8,128)(2,1)} %points_ref.3), custom_call_target="tpu_custom_call" | custom-call | tf_op jit(solution)/shard_map/gather/pallas_call | solution.py:357
  26.8 0.5 slice.3
  28.0 0.0 copy-start
  28.0 0.7 copy-done
  28.7 32.8 %factor.1 = (bf16[1024,1024]{1,0:T(8,128)(2,1)S(1)}, bf16[1024,1024]{1,0:T(8,128)(2,1)S(1)}, f32[8,1024]{1,0:T(8,128)S(1)}) custom-call(bf16[1024,256]{1,0:T(8,128)(2,1)S(1)} %get-tuple-element.45.marks_ref, f32[1,1024]{1,0:T(1,128)S(1)} %bitcast.9), custom_call_target="tpu_custom_call" | custom-call | tf_op jit(solution)/shard_map/factor/pallas_call | solution.py:181
  61.5 23.8 %raw.1 = (f32[2048,1024]{1,0:T(8,128)S(1)}, f32[16,128]{1,0:T(8,128)S(1)}) custom-call(bf16[2048,256]{1,0:T(8,128)(2,1)} %get-tuple-element.127, bf16[1024,256]{1,0:T(8,128)(2,1)S(1)} %get-tuple-element.45.marks_ref, f32[8,1024]{1,0:T(8,128)S(1)} %get-tuple-element.46.norm_ref, bf16[1024,1024]{1,0:T(8,128)(2,1)S(1)} %get-tuple-element.47.hi_ref, ...), custom_call_target="tpu_custom_call" | custom-call | tf_op jit(solution)/shard_map/raw/pallas_call | solution.py:476
  85.3 4.0 %standardize.1 = bf16[2048,1024]{1,0:T(8,128)(2,1)} custom-call(f32[2048,1024]{1,0:T(8,128)S(1)} %get-tuple-element.49.raw_ref, f32[16,128]{1,0:T(8,128)S(1)} %get-tuple-element.50.stats_ref), custom_call_target="tpu_custom_call" | custom-call | tf_op jit(solution)/shard_map/standardize/pallas_call | solution.py:515
  (2 shorter events, 0.0 us)
Async XLA Ops:
  28.0 0.7 copy-start

commit v7 on v6

--- a/solution.py
+++ b/solution.py
@@ -197,7 +197,7 @@
         ],
         name="factor",
         compiler_params=pltpu.CompilerParams(vmem_limit_bytes=40 << 20),
-    )(marks, ridge.reshape(1, n))
+    )(marks, ridge)
 
 
 MESH_IDS = pl.DeviceIdType.MESH
@@ -251,12 +251,15 @@
 
 
 def gather_kernel(
-    ids_ref, turn_ref, points_ref, marks_ref, over_ref, pts, rows, line, window, windows, hot, s0, s1, r1, s2, r2, s3, r3
+    ids_ref, turn_ref, points_ref, ridge_ref, marks_ref, over_ref, near_ref, pts, rows, line, window, windows, hot,
+    s0, s1, r1, s2, r2, s3, r3
 ):
     inner, outer = position()
     core = lax.rem(inner, 2)
-    fetch = pltpu.make_async_copy(points_ref, pts, s0)
+    fetch = pltpu.make_async_copy(points_ref, pts, s0.at[0])
     fetch.start()
+    fetch_ridge = pltpu.make_async_copy(ridge_ref, near_ref, s0.at[1])
+    fetch_ridge.start()
     barrier = greet(inner, outer)
     count, d = points_ref.shape
     n = marks_ref.shape[0]
@@ -274,6 +277,7 @@
     sel = jnp.sum(jnp.where(wanted, ids - start + 1, 0).astype(F32), axis=1, keepdims=True) - 1.0
     pick = (iota((SLOTS, count), 1).astype(F32) == sel).astype(BF16)
     fetch.wait()
+    fetch_ridge.wait()
     picked = jnp.dot(pick, pts[...], preferred_element_type=F32).astype(BF16)
     rows[0] = picked[:, :128]
     rows[1] = picked[:, 128:]
@@ -351,14 +355,18 @@
         marks_ref[part, :] = jnp.dot(hot[part, :], source, preferred_element_type=F32).astype(BF16)
 
 
-def gather_turn(ids, turn, points):
+def gather_turn(ids, turn, points, ridge):
     d = points.shape[1]
     n = ids.shape[1]
     return pl.pallas_call(
         gather_kernel,
-        out_shape=[jax.ShapeDtypeStruct((n, d), BF16), jax.ShapeDtypeStruct((8, 128), jnp.int32)],
-        in_specs=[VMEM, VMEM, pl.BlockSpec(memory_space=pl.ANY)],
-        out_specs=[VMEM, VMEM],
+        out_shape=[
+            jax.ShapeDtypeStruct((n, d), BF16),
+            jax.ShapeDtypeStruct((8, 128), jnp.int32),
+            jax.ShapeDtypeStruct((1, n), F32),
+        ],
+        in_specs=[VMEM, VMEM, pl.BlockSpec(memory_space=pl.ANY), pl.BlockSpec(memory_space=pl.ANY)],
+        out_specs=[VMEM, VMEM, VMEM],
         scratch_shapes=[
             pltpu.VMEM(points.shape, BF16),
             pltpu.VMEM((2, SLOTS, d // 2), BF16),
@@ -366,33 +374,34 @@
             pltpu.VMEM((WINDOW, d // 2), BF16),
             pltpu.VMEM((2, 16, WINDOW, d // 2), BF16),
             pltpu.VMEM((n, 16 * WINDOW), BF16),
-            DMA,
+            DMA((2,)),
         ]
         + [DMA((16,))] * 6,
         name="gather",
         compiler_params=pltpu.CompilerParams(
             collective_id=0, has_side_effects=True, vmem_limit_bytes=24 << 20
         ),
-    )(ids, turn, points)
-
-
-def gather_marks(points, ids):
+    )(ids, turn, points, ridge)
+
+
+def gather_marks(points, ids, ridge):
     n = ids.shape[0]
     ids = ids.reshape(1, n)
+    ridge = ridge.reshape(1, n)
     place = jnp.arange(n, dtype=jnp.int32)[:, None]
 
     def turn(low, high):
         bounds = jnp.stack([low, high]).astype(jnp.int32)
-        return gather_turn(ids, jnp.broadcast_to(bounds[:, None], (2, 128)), points)
-
-    marks, over = turn(jnp.int32(0), jnp.int32(n))
+        return gather_turn(ids, jnp.broadcast_to(bounds[:, None], (2, 128)), points, ridge)
+
+    marks, over, near = turn(jnp.int32(0), jnp.int32(n))
 
     def again(state):
         low, marks = state
         fresh = turn(low, low + SLOTS)[0]
         return low + SLOTS, jnp.where((place >= low) & (place < low + SLOTS), fresh, marks)
 
-    return lax.while_loop(lambda s: s[0] < n, again, (jnp.where(over[0, 0] > 0, 0, n), marks))[1]
+    return lax.while_loop(lambda s: s[0] < n, again, (jnp.where(over[0, 0] > 0, 0, n), marks))[1], near
 
 
 def raw_kernel(
@@ -524,7 +533,7 @@
 
 
 def shards(points, ridge, landmark_ids):
-    marks = gather_marks(points, landmark_ids)
+    marks, ridge = gather_marks(points, landmark_ids, ridge)
     hi, lo, norms = factor(marks, ridge)
     raw, stats = raw_features(points, marks, norms, hi, lo, points.shape[0] * lax.axis_size(GRP_DEV))
     return standardize(raw, stats)

time: 89.7 us -> 89 us (level)
  no operation moved by 1% of the time
where the time goes in v7:
time: 89 us; the launch traced here: 88.8 us
  Pallas kernels  87.4 us (98%)
    pallas_call x1, Pallas kernels, factor(): pl.pallas_call(factor_kernel, out_shape=[jax.ShapeDtypeStruct((n, n), BF1...  32.8 us
    pallas_call x1, Pallas kernels, gather_turn(): pl.pallas_call(gather_kernel, out_shape=[jax.ShapeDtypeStruct((n, d), BF1...  26.8 us
    pallas_call x1, Pallas kernels, raw_features(): pl.pallas_call(functools.partial(raw_kernel, rows_total), out_shape=[jax....  23.8 us
    pallas_call x1, Pallas kernels, standardize(): pl.pallas_call(standardize_kernel, out_shape=jax.ShapeDtypeStruct((rows,...  3.99 us

profile of v7, /device:TPU:1, one launch (start us, length us, event | category | flops | bytes accessed | tf_op | source)
XLA Modules:
  0.0 88.8 jit_solution(4236451543127222184)
XLA Ops:
  0.0 0.1 broadcast_in_dim.29.turn_ref
  0.1 26.8 %gather.2 = (bf16[1024,256]{1,0:T(8,128)(2,1)S(1)}, s32[8,128]{1,0:T(8,128)S(1)}, f32[1,1024]{1,0:T(1,128)S(1)}) custom-call(s32[1,1024]{1,0:T(1,128)} %bitcast.9, s32[2,128]{1,0:T(2,128)S(1)} %broadcast_in_dim.29.turn_ref, bf16[2048,256]{1,0:T(8,128)(2,1)} %points_ref.3, f32[1,1024]{1,0:T(1,128)} %bitcast.11), custom_call_target="tpu_custom_call" | custom-call | tf_op jit(solution)/shard_map/gather/pallas_call | solution.py:361
  26.9 0.5 slice.3
  28.1 32.8 %factor.1 = (bf16[1024,1024]{1,0:T(8,128)(2,1)S(1)}, bf16[1024,1024]{1,0:T(8,128)(2,1)S(1)}, f32[8,1024]{1,0:T(8,128)S(1)}) custom-call(bf16[1024,256]{1,0:T(8,128)(2,1)S(1)} %get-tuple-element.51.marks_ref, f32[1,1024]{1,0:T(1,128)S(1)} %get-tuple-element.52.ridge_ref), custom_call_target="tpu_custom_call" | custom-call | tf_op jit(solution)/shard_map/factor/pallas_call | solution.py:181
  60.8 23.8 %raw.1 = (f32[2048,1024]{1,0:T(8,128)S(1)}, f32[16,128]{1,0:T(8,128)S(1)}) custom-call(bf16[2048,256]{1,0:T(8,128)(2,1)} %get-tuple-element.149, bf16[1024,256]{1,0:T(8,128)(2,1)S(1)} %get-tuple-element.51.marks_ref, f32[8,1024]{1,0:T(8,128)S(1)} %get-tuple-element.53.norm_ref, bf16[1024,1024]{1,0:T(8,128)(2,1)S(1)} %get-tuple-element.54.hi_ref, ...), custom_call_target="tpu_custom_call" | custom-call | tf_op jit(solution)/shard_map/raw/pallas_call | solution.py:485
  84.7 4.0 %standardize.1 = bf16[2048,1024]{1,0:T(8,128)(2,1)} custom-call(f32[2048,1024]{1,0:T(8,128)S(1)} %get-tuple-element.56.raw_ref, f32[16,128]{1,0:T(8,128)S(1)} %get-tuple-element.57.stats_ref), custom_call_target="tpu_custom_call" | custom-call | tf_op jit(solution)/shard_map/standardize/pallas_call | solution.py:524
  (2 shorter events, 0.0 us)

commit v8 on v7

--- a/solution.py
+++ b/solution.py
@@ -13,7 +13,7 @@
 BF16 = jnp.bfloat16
 HI = lax.Precision.HIGHEST
 BLK = 128
-ROWS_STEP = 1024
+ROWS_STEP = 512
 OUT_STEP = 256
 VMEM = pl.BlockSpec(memory_space=pltpu.VMEM)
 
@@ -421,7 +421,7 @@
     own[...] = jnp.zeros_like(own)
 
     def block(i, carry):
-        here = pl.ds(pl.multiple_of(i * ROWS_STEP, ROWS_STEP), ROWS_STEP)
+        here = slice(i * ROWS_STEP, (i + 1) * ROWS_STEP)
         pts = points_ref[here, :]
         nc = jnp.sum(jnp.square(pts.astype(F32)), axis=1, keepdims=True)
         g = lax.dot_general(pts, marks_ref[...], (((1,), (1,)), ((), ())), preferred_element_type=F32)
@@ -443,7 +443,8 @@
                 own[1, r : r + 1, :] += jnp.sum(jnp.square(y), axis=0, keepdims=True)
         return carry
 
-    lax.fori_loop(0, rows // ROWS_STEP, block, 0)
+    for i in range(rows // ROWS_STEP):
+        block(i, 0)
     line[inner] = own[core]
     pl.semaphore_wait(barrier, 45)
 

time: 89 us -> 88.9 us (level)
  no operation moved by 1% of the time
where the time goes in v8:
time: 88.9 us; the launch traced here: 88.8 us
  Pallas kernels  87.1 us (98%)
    pallas_call x1, Pallas kernels, factor(): pl.pallas_call(factor_kernel, out_shape=[jax.ShapeDtypeStruct((n, n), BF1...  32.8 us
    pallas_call x1, Pallas kernels, gather_turn(): pl.pallas_call(gather_kernel, out_shape=[jax.ShapeDtypeStruct((n, d), BF1...  26.8 us
    pallas_call x1, Pallas kernels, raw_features(): pl.pallas_call(functools.partial(raw_kernel, rows_total), out_shape=[jax....  23.5 us
    pallas_call x1, Pallas kernels, standardize(): pl.pallas_call(standardize_kernel, out_shape=jax.ShapeDtypeStruct((rows,...  3.99 us

profile of v8, /device:TPU:1, one launch (start us, length us, event | category | flops | bytes accessed | tf_op | source)
XLA Modules:
  0.0 88.8 jit_solution(3852441175423907070)
XLA Ops:
  0.0 0.1 broadcast_in_dim.29.turn_ref
  0.1 26.8 %gather.2 = (bf16[1024,256]{1,0:T(8,128)(2,1)S(1)}, s32[8,128]{1,0:T(8,128)S(1)}, f32[1,1024]{1,0:T(1,128)S(1)}) custom-call(s32[1,1024]{1,0:T(1,128)} %bitcast.9, s32[2,128]{1,0:T(2,128)S(1)} %broadcast_in_dim.29.turn_ref, bf16[2048,256]{1,0:T(8,128)(2,1)} %points_ref.3, f32[1,1024]{1,0:T(1,128)} %bitcast.11), custom_call_target="tpu_custom_call" | custom-call | tf_op jit(solution)/shard_map/gather/pallas_call | solution.py:361
  26.9 0.5 slice.3
  28.0 0.2 while.12
  28.2 32.8 %factor.1 = (bf16[1024,1024]{1,0:T(8,128)(2,1)S(1)}, bf16[1024,1024]{1,0:T(8,128)(2,1)S(1)}, f32[8,1024]{1,0:T(8,128)S(1)}) custom-call(bf16[1024,256]{1,0:T(8,128)(2,1)S(1)} %get-tuple-element.51.marks_ref, f32[1,1024]{1,0:T(1,128)S(1)} %get-tuple-element.52.ridge_ref), custom_call_target="tpu_custom_call" | custom-call | tf_op jit(solution)/shard_map/factor/pallas_call | solution.py:181
  61.1 23.5 %raw.1 = (f32[2048,1024]{1,0:T(8,128)S(1)}, f32[16,128]{1,0:T(8,128)S(1)}) custom-call(bf16[2048,256]{1,0:T(8,128)(2,1)} %get-tuple-element.149, bf16[1024,256]{1,0:T(8,128)(2,1)S(1)} %get-tuple-element.51.marks_ref, f32[8,1024]{1,0:T(8,128)S(1)} %get-tuple-element.53.norm_ref, bf16[1024,1024]{1,0:T(8,128)(2,1)S(1)} %get-tuple-element.54.hi_ref, ...), custom_call_target="tpu_custom_call" | custom-call | tf_op jit(solution)/shard_map/raw/pallas_call | solution.py:486
  84.6 4.0 %standardize.1 = bf16[2048,1024]{1,0:T(8,128)(2,1)} custom-call(f32[2048,1024]{1,0:T(8,128)S(1)} %get-tuple-element.56.raw_ref, f32[16,128]{1,0:T(8,128)S(1)} %get-tuple-element.57.stats_ref), custom_call_target="tpu_custom_call" | custom-call | tf_op jit(solution)/shard_map/standardize/pallas_call | solution.py:525
  (1 shorter events, 0.0 us)
